TPU v7x, 256 devices: a whole 4x4x8 slice. The times are simulated.
256 devices in a mesh: view: 4 (over y), sent: 32 (over x, z), col: 2 (over core).
Axes of the slice: x: 4, y: 4, z: 8, core: 2. Of those that a mesh axis runs over, the one named last changes fastest.
Arguments:
- sketched: bfloat16 [12, 32768, 2048], P('view', 'sent', 'col')
- widths: int32 [12], P('view'), may hold values from 256 to 2048, as said below
- inv_factor: float32 [12, 2048, 2048], P('view', 'sent', 'col'), as said below
- shared: bfloat16 [32768, 256], P('sent'), may hold values from -6 to 6
Outputs:
- loadings: float32 [12, 2048, 256], P('view', 'col')
- updated: float32 [32768, 256], P('sent')
Inputs may be any that keep to these rules, and one draw needn't show every extreme that they name: `widths`: every width is a multiple of 128; in every draw one view has width 2048 and another 2 * 128. Each inv_factor[j] is lower triangular with diagonal entries of 1 to 2.
All inputs are finite; a program needn't handle non-finite values.
Results may differ from a plain program's by a relative error of at most 0.0026.
Values sent between devices are 32-bit elements; how exact they have to be, the bound alone decides.
A program may use at most 128 MiB of HBM per device.

v0:
```python
import math

import jax
import jax.numpy as jnp
from jax import lax
from jax.sharding import PartitionSpec as P


def shards(sketched, widths, inv_factor, shared):
    view_count, row_count, col_half = sketched.shape
    factor_rows = inv_factor.shape[1]
    total_rows = row_count * lax.axis_size("sent")
    scale = 1.0 / math.sqrt(total_rows)
    high = lax.Precision.HIGHEST
    col_index = lax.axis_index("col")
    sent_index = lax.axis_index("sent")
    col_pos = col_index * col_half + jnp.arange(col_half)
    keep_cols = (col_pos[None, :] < widths[:, None]).astype(jnp.float32)[:, :, None]
    row_pos = sent_index * factor_rows + jnp.arange(factor_rows)
    keep_rows = (row_pos[None, :] < widths[:, None]).astype(jnp.float32)[:, :, None]
    terms = jnp.einsum("vrd,rk->vdk", sketched, shared, preferred_element_type=jnp.float32) * scale
    proj = lax.psum(terms, "sent") * keep_cols
    half_part = jnp.einsum("vid,vdk->vik", inv_factor, proj, precision=high)
    half = lax.psum(half_part, "col") * keep_rows
    back = jnp.einsum("vid,vik->vdk", inv_factor, half, precision=high)
    loadings = lax.psum(back, "sent") * keep_cols
    wload = loadings.astype(jnp.bfloat16)
    contrib = jnp.einsum("vrd,vdk->rk", sketched, wload, preferred_element_type=jnp.float32)
    merged = lax.psum(contrib, ("view", "col"))
    local_gram = lax.dot_general(merged, merged, (((0,), (0,)), ((), ())), precision=high)
    gram = lax.psum(local_gram, "sent")
    lower = jnp.linalg.cholesky(gram)
    updated = lax.linalg.triangular_solve(
        lower, merged, left_side=False, lower=True, transpose_a=True
    ) * math.sqrt(total_rows)
    return (loadings, updated)


def solution(mesh):
    return jax.shard_map(
        shards,
        mesh=mesh,
        in_specs=(P("view", "sent", "col"), P("view"), P("view", "sent", "col"), P("sent", None)),
        out_specs=(P("view", "col", None), P("sent", None)),
        check_vma=False,
    )
```

profile of v0, /device:TPU:1, one launch (start us, length us, event | category | flops | bytes accessed | tf_op | source)
XLA Modules:
  0.0 661.3 jit_solution(16544654213980719172)
XLA Ops:
  7.2 6.7 %convolution_multiply_fusion = f32[3,1024,256]{1,2,0:T(8,128)} fusion(bf16[3,1024,1024]{2,1,0:T(8,128)(2,1)} %param.4, bf16[1024,256]{1,0:T(8,128)(2,1)} %param.7), kind=kOutput, calls=%fused_computation.5 | convolution fusion | flops 1611399168 | bytes 9961472 | tf_op jit(solution)/shard_map/vrd,rk->vdk/dot_general | solution.py:21
  14.0 0.5 copy-done.3
  14.6 157.6 %all-reduce.7.cloned.1.call-done = f32[3,1024,256]{1,2,0:T(8,128)} async-done(((f32[3,1024,256]{1,2,0:T(8,128)}), f32[3,1024,256]{1,2,0:T(8,128)}) %all-reduce.7.cloned.1.call-update) | async-done | bytes 3145744 | tf_op jit(solution)/shard_map/psum | solution.py:22
  172.2 5.7 fusion.8
  178.1 30.2 %all-reduce.9.cloned.1.call-done = f32[3,64,256]{2,1,0:T(8,128)} async-done(((f32[3,64,256]{2,1,0:T(8,128)}), f32[3,64,256]{2,1,0:T(8,128)}) %all-reduce.9.cloned.1.call-update) | async-done | bytes 196624 | tf_op jit(solution)/shard_map/psum | solution.py:24
  208.4 5.3 convolution_bitcast_fusion
  213.7 155.1 %all-reduce.11.cloned.1.call-done = f32[3,1024,256]{1,2,0:T(8,128)} async-done(((f32[3,1024,256]{1,2,0:T(8,128)}), f32[3,1024,256]{1,2,0:T(8,128)}) %all-reduce.11.cloned.1.call-update) | async-done | bytes 3145744 | tf_op jit(solution)/shard_map/psum | solution.py:26
  368.9 2.2 broadcast_multiply_fusion
  371.1 1.7 copy-done.1
  372.8 5.7 fusion.5
  378.4 0.2 all-reduce.15.cloned.1.call-start
  378.7 66.1 %all-reduce.13.cloned.1.call-done = f32[1024,256]{0,1:T(8,128)} async-done(((f32[1024,256]{0,1:T(8,128)}), f32[1024,256]{0,1:T(8,128)}) %all-reduce.13.cloned.1.call-update) | async-done | bytes 1048592 | tf_op jit(solution)/shard_map/psum | solution.py:29
  444.8 3.3 fusion.23
  448.1 3.5 copy.8
  451.7 138.0 %all-reduce.15.cloned.1.call-done = f32[256,256]{0,1:T(8,128)} async-done(((f32[256,256]{0,1:T(8,128)}), f32[256,256]{0,1:T(8,128)}) %all-reduce.15.cloned.1.call-update) | async-done | bytes 262160 | tf_op jit(solution)/shard_map/psum | solution.py:31
  589.6 1.1 copy.7
  590.7 1.0 fusion.14
  591.7 11.7 %cholesky.50 = f32[128,128]{1,0:T(8,128)S(1)} custom-call(f32[128,128]{1,0:T(8,128)S(1)} %cholesky.118), custom_call_target="Cholesky" | custom-call | tf_op jit(solution)/shard_map/jit(cholesky)/cholesky | solution.py:32
  603.5 9.8 %custom-call.14 = f32[1,128,128]{1,2,0:T(8,128)S(1)} custom-call(f32[1,128,128]{2,1,0:T(8,128)S(1)} %get-tuple-element.25), custom_call_target="InvertDiagBlocksLowerTriangular" | custom-call | tf_op jit(solution)/shard_map/jit(cholesky)/cholesky | solution.py:32
  613.5 0.3 convolution_subtract_fusion.1
  613.8 11.7 %cholesky.105 = f32[128,128]{1,0:T(8,128)S(1)} custom-call(f32[128,128]{1,0:T(8,128)S(1)} %convolution_subtract_fusion.1), custom_call_target="Cholesky" | custom-call | tf_op jit(solution)/shard_map/jit(cholesky)/cholesky | solution.py:32
  625.5 0.7 compare_reduce_fusion
  627.6 3.9 while.1
  627.6 0.6 fusion.35
  628.2 1.4 bitcast_dynamic-update-slice_fusion.2
  629.6 0.6 fusion.35
  630.1 1.4 bitcast_dynamic-update-slice_fusion.2
  631.5 19.9 %custom-call.15 = f32[2,128,128]{1,2,0:T(8,128)S(1)} custom-call(f32[2,128,128]{2,1,0:T(8,128)S(1)} %get-tuple-element.9), custom_call_target="InvertDiagBlocksLowerTriangular" | custom-call | tf_op jit(solution)/shard_map/triangular_solve | solution.py:33
  651.4 0.6 fusion.11
  652.0 0.6 convolution_subtract_fusion
  652.7 0.6 fusion.17
  653.4 1.3 copy.9
  (31 shorter events, 1.0 us)
Async XLA Ops:
  7.2 165.1 %copy-start = (f32[3,64,1024]{2,1,0:T(8,128)S(1)}, f32[3,64,1024]{2,1,0:T(8,128)}, u32[]{:S(2)}) copy-start(f32[3,64,1024]{2,1,0:T(8,128)} %param.6) | copy-start | bytes 2359300
  7.2 165.1 %all-reduce.7.cloned.1.call-start = ((), (), s32[]{:S(2)}) async-start(), calls=%async_computation | async-start | bytes 6291456 | tf_op jit(solution)/shard_map/psum | solution.py:22
  13.9 0.7 copy-start.3
  13.9 194.4 %all-reduce.9.cloned.1.call-start = ((), (), s32[]{:S(2)}) async-start(), calls=%async_computation.1 | async-start | bytes 393216 | tf_op jit(solution)/shard_map/psum | solution.py:24
  178.0 190.9 %all-reduce.11.cloned.1.call-start = ((), (), s32[]{:S(2)}) async-start(), calls=%async_computation.2 | async-start | bytes 6291456 | tf_op jit(solution)/shard_map/psum | solution.py:26
  213.7 231.1 %all-reduce.13.cloned.1.call-start = ((), (), s32[]{:S(2)}) async-start(), calls=%async_computation.3 | async-start | bytes 2097152 | tf_op jit(solution)/shard_map/psum | solution.py:29
  371.1 1.7 copy-start.1
  378.4 211.2 %all-reduce.15.cloned.1.call-start = ((), (), s32[]{:S(2)}) async-start(), calls=%async_computation.4 | async-start | bytes 524288 | tf_op jit(solution)/shard_map/psum | solution.py:31
  451.7 199.7 %copy-start.2 = (f32[1024,256]{0,1:T(8,128)S(1)}, f32[1024,256]{0,1:T(8,128)}, u32[]{:S(2)}) copy-start(f32[1024,256]{0,1:T(8,128)} %all-reduce.13.cloned.1.call-done) | copy-start | bytes 3145732
Sparse Core Ops, SparseCore 0:
  14.1 158.1 all-reduce.6
  178.1 30.1 all-reduce.8
  213.8 155.0 all-reduce.10
  378.6 66.1 all-reduce.12
  448.7 140.9 all-reduce.14
where the time goes:
time: 665 us; the launch traced here: 661 us
  waiting for transfers between devices  547 us (82%)
  other arithmetic  57.4 us (9%)
  matrix products  29 us (4%)
  between operations  15.2 us (2%)
  local copies, waits for them, and re-layouts  12.1 us (2%)
    psum x1, waiting for transfers between devices, shards(): proj = lax.psum(terms, 'sent') * keep_cols  158 us
    psum x1, waiting for transfers between devices, shards(): loadings = lax.psum(back, 'sent') * keep_cols  155 us
    psum x1, waiting for transfers between devices, shards(): gram = lax.psum(local_gram, 'sent')  138 us
    psum x1, waiting for transfers between devices, shards(): merged = lax.psum(contrib, ('view', 'col'))  66.1 us
    another operation x6, other arithmetic, shards(): lower = jnp.linalg.cholesky(gram)  34 us
    psum x1, waiting for transfers between devices, shards(): half = lax.psum(half_part, 'col') * keep_rows  30.2 us
    another operation x3, other arithmetic, shards(): lax.linalg.triangular_solve(lower, merged, left_side=False, lower=True, t...  19.9 us
  transfers between devices with their start and end apart: 5, of which 5 were waited for; matrix products, arithmetic and copies ran while one was open for 1% of the time, Pallas kernels for 0%

commit v1 on v0

v1 whole, which is shorter than its diff:
```python
import math

import jax
import jax.numpy as jnp
from jax import lax
from jax.experimental import pallas as pl
from jax.experimental.pallas import tpu as pltpu
from jax.sharding import PartitionSpec as P

MESH = pl.DeviceIdType.MESH
HIGH = lax.Precision.HIGHEST
F32 = jnp.float32
BF16 = jnp.bfloat16
NX, NZ, NY = 4, 8, 4
SEMS = 256


class Links:
    def __init__(self, send_sems, recv_sems):
        self.send_sems, self.recv_sems, self.used, self.sent = send_sems, recv_sems, 0, []

    def slot(self):
        self.used += 1
        assert self.used <= SEMS
        return self.used - 1

    def copy(self, slot, src, dst, device):
        return pltpu.make_async_remote_copy(
            src_ref=src, dst_ref=dst, send_sem=self.send_sems.at[slot], recv_sem=self.recv_sems.at[slot],
            device_id=device, device_id_type=MESH)

    def send(self, slot, src, dst, device):
        made = self.copy(slot, src, dst, device)
        made.start()
        self.sent.append(made)

    def arrived(self, slot, dst, device):
        self.copy(slot, dst, dst, device).wait_recv()

    def drain(self):
        for made in self.sent:
            made.wait_send()
        self.sent = []


class Ring:
    def __init__(self, links, size, pos, device):
        self.links, self.size, self.pos, self.device = links, size, pos, device

    def at(self, delta):
        return lax.rem(self.pos + (delta % self.size), self.size)


class ReduceScatter:
    def __init__(self, ring, own, landing):
        self.ring, self.own, self.landing = ring, own, landing
        self.half_ring = ring.size // 2
        self.slots = {(d, kind, t): ring.links.slot()
                      for t in range(1, self.half_ring + 1) for d in (0, 1) for kind in (0, 1)
                      if not (kind == 1 and t == self.half_ring)}

    def wait(self, d, kind, t):
        sign = (-1, 1)[d]
        buf = self.landing.at[d, kind, t - 1]
        self.ring.links.arrived(self.slots[d, kind, t], buf, self.ring.device(sign))
        return buf

    def step(self, t):
        for kind in (0, 1):
            for d, sign in ((0, -1), (1, 1)):
                if (d, kind, t) not in self.slots:
                    continue
                dist = self.half_ring + 1 - t - kind
                mine = self.own(self.ring.at(sign * dist), d if kind == 0 else 1 - d)
                if t == 1:
                    src = mine
                else:
                    src = self.wait(d, kind, t - 1)
                    src[...] = src[...] + mine[...]
                self.ring.links.send(self.slots[d, kind, t], src, self.landing.at[d, kind, t - 1],
                                     self.ring.device(sign))

    def final(self):
        last = self.half_ring
        out = []
        for h in (0, 1):
            far = self.wait(h, 0, last)
            near = self.wait(1 - h, 1, last - 1)
            out.append(self.own(self.ring.pos, h)[...] + far[...] + near[...])
        return out


class AllGather:
    def __init__(self, ring, full, half):
        self.ring, self.full, self.half = ring, full, half
        self.half_ring = ring.size // 2
        self.slots = {(d, t): ring.links.slot() for t in range(1, self.half_ring + 1) for d in (0, 1)}

    def view(self, d, t, owner):
        return self.half(owner, d) if t == self.half_ring else self.full(owner)

    def wait(self, d, t):
        sign = (-1, 1)[d]
        dst = self.view(d, t, self.ring.at(-sign * t))
        self.ring.links.arrived(self.slots[d, t], dst, self.ring.device(sign))

    def step(self, t):
        for d, sign in ((0, -1), (1, 1)):
            if t > 1:
                self.wait(d, t - 1)
            src = self.view(d, t, self.ring.at(-sign * (t - 1)))
            self.ring.links.send(self.slots[d, t], src, src, self.ring.device(sign))

    def final(self):
        for d in (0, 1):
            self.wait(d, self.half_ring)


def place():
    y, s, c = lax.axis_index("view"), lax.axis_index("sent"), lax.axis_index("col")
    return y, s // NZ, lax.rem(s, NZ), c


def rings(links, x, z, y):
    def x_dev(sign):
        return {"sent": lax.rem(x + (sign % NX), NX) * NZ + z}

    def z_dev(sign):
        return {"sent": x * NZ + lax.rem(z + (sign % NZ), NZ)}

    def y_dev(sign):
        return {"view": lax.rem(y + (sign % NY), NY)}

    return Ring(links, NX, x, x_dev), Ring(links, NZ, z, z_dev), Ring(links, NY, y, y_dev)


def greet(devices):
    barrier = pltpu.get_barrier_semaphore()
    for device in devices:
        pl.semaphore_signal(barrier, inc=1, device_id=device, device_id_type=MESH)
    pl.semaphore_wait(barrier, len(devices))


def nt(a, b):
    return lax.dot_general(a, b, (((1,), (1,)), ((), ())), precision=HIGH, preferred_element_type=F32)


def nn(a, b):
    return lax.dot_general(a, b, (((1,), (0,)), ((), ())), precision=HIGH, preferred_element_type=F32)


def project(scale, widths, shared, inv, sketched, loadings, contrib,
            feats, sharedT, terms, land_x, quarter, land_z, land_z2, quarter2, land_x2, proj, invx,
            part, part_in, part_sum, land_h, half, back, land_b, loadT, stage,
            send_sems, recv_sems, feat_sems, out_sems, own_sem):
    y, x, z, c = place()
    links = Links(send_sems, recv_sems)
    rx, rz, _ = rings(links, x, z, y)
    partner = {"col": 1 - c}
    across = {"sent": lax.rem(x + 2, NX) * NZ + z}

    quarters = [lax.rem(x + d, NX) for d in (2, 3, 1, 0)]
    loads = {}
    for i, v in enumerate((2, 0, 1)):
        for n, q in enumerate(quarters):
            loads[v, n] = pltpu.make_async_copy(
                sketched.at[v, :, pl.ds(pl.multiple_of(q * 256, 256), 256)], feats.at[v, q],
                feat_sems.at[4 * i + n])
            loads[v, n].start()
    own_inv = pltpu.make_async_copy(
        inv.at[:, :, pl.ds(pl.multiple_of(x * 256, 256), 256)], invx.at[:, x], own_sem)
    own_inv.start()
    sharedT[...] = shared[...].T

    greet([rx.device(-1), rx.device(1), rz.device(-1), rz.device(1), across, partner])

    def make_terms(v):
        for n, q in enumerate(quarters):
            loads[v, n].wait()
            terms[v, q] = jnp.dot(sharedT[...], feats[v, q], preferred_element_type=F32).reshape(NZ, 32, 256)

    xs = [ReduceScatter(rx, lambda o, h, v=v: terms.at[v, o, pl.ds(4 * h, 4)], land_x.at[v]) for v in (0, 1)]
    zs = [ReduceScatter(rz, lambda o, h, v=v: quarter.at[v, o, pl.ds(16 * h, 16)], land_z.at[v]) for v in (0, 1)]
    z2 = ReduceScatter(rz, lambda o, h: terms.at[2, :, o, pl.ds(16 * h, 16)], land_z2)
    x2 = ReduceScatter(rx, lambda o, h: quarter2.at[o, pl.ds(16 * h, 16)], land_x2)

    def lanes_kept(v, first, value):
        col = first + lax.broadcasted_iota(jnp.int32, value.shape, 1)
        return jnp.where(col < widths[v], value, 0.0)

    first_col = c * 1024 + x * 256

    def own_proj(v, halves):
        for h in (0, 1):
            proj[z, v, pl.ds(16 * h, 16)] = lanes_kept(v, first_col, halves[h] * scale)

    def own_quarter(v):
        halves = xs[v].final()
        for h in (0, 1):
            quarter[v, pl.ds(4 * h, 4)] = halves[h]

    make_terms(2)
    z2.step(1)
    make_terms(0)
    xs[0].step(1)
    make_terms(1)
    xs[1].step(1)
    z2.step(2)
    xs[0].step(2)
    z2.step(3)
    xs[1].step(2)
    own_quarter(0)
    zs[0].step(1)
    z2.step(4)
    zs[0].step(2)
    own_quarter(1)
    zs[1].step(1)
    halves = z2.final()
    for h in (0, 1):
        quarter2[:, pl.ds(16 * h, 16)] = halves[h]
    x2.step(1)
    zs[0].step(3)
    zs[1].step(2)
    x2.step(2)
    inv_slots = {d: links.slot() for d in (1, 3, 2)}
    inv_dev = {1: rx.device(1), 3: rx.device(-1), 2: across}
    for d in (1, 3, 2):
        q = rx.at(d)
        links.send(inv_slots[d], inv.at[:, :, pl.ds(pl.multiple_of(q * 256, 256), 256)], invx.at[:, x], inv_dev[d])
    zs[0].step(4)
    zs[1].step(3)
    own_proj(2, x2.final())
    own_proj(0, zs[0].final())
    zs[1].step(4)
    own_proj(1, zs[1].final())

    gather = AllGather(rz, lambda o: proj.at[o], lambda o, h: proj.at[o, :, pl.ds(16 * h, 16)])
    for t in range(1, 5):
        gather.step(t)
    own_inv.wait()
    for d in (1, 3, 2):
        links.arrived(inv_slots[d], invx.at[:, rx.at(-d)], inv_dev[d])
    gather.final()

    for v in range(3):
        product = nt(proj[:, v].reshape(256, 256), invx[v].reshape(256, 256)).reshape(2, NX, 32, 256)
        part[:, :, v] = product
    slot = links.slot()
    links.send(slot, part.at[1 - c], part_in, partner)
    links.arrived(slot, part_in, partner)
    part_sum[...] = part[c] + part_in[...]
    hs = ReduceScatter(rx, lambda o, h: part_sum.at[o, :, pl.ds(16 * h, 16)], land_h)
    hs.step(1)
    hs.step(2)
    halves = hs.final()
    lane = lax.broadcasted_iota(jnp.int32, (16, 256), 1)
    row = (lane // 64) * (64 * NZ) + z * 64 + lax.rem(lane, 64)
    for h in (0, 1):
        for v in range(3):
            half[c, x, v, pl.ds(16 * h, 16)] = jnp.where(row < widths[v], halves[h][v], 0.0)
    hg = AllGather(rx, lambda o: half.at[c, o], lambda o, h: half.at[c, o, :, pl.ds(16 * h, 16)])
    hg.step(1)
    hg.step(2)
    hg.final()
    slot = links.slot()
    links.send(slot, half.at[c], half.at[c], partner)
    links.arrived(slot, half.at[1 - c], partner)

    for v in range(3):
        back[:, v] = nn(half[:, :, v].reshape(256, 256), invx[v].reshape(256, 256)).reshape(NZ, 32, 256)
    bs = ReduceScatter(rz, lambda o, h: back.at[o, :, pl.ds(16 * h, 16)], land_b)
    for t in range(1, 5):
        bs.step(t)
    halves = bs.final()
    for h in (0, 1):
        for v in range(3):
            loadT[v, x, z, pl.ds(16 * h, 16)] = lanes_kept(v, first_col, halves[h][v])

    gz = AllGather(rz, lambda o: loadT.at[pl.ds(0, 2), x, o], lambda o, h: loadT.at[pl.ds(0, 2), x, o, pl.ds(16 * h, 16)])
    gx = AllGather(rx, lambda o: loadT.at[pl.ds(0, 2), o], lambda o, h: loadT.at[pl.ds(0, 2), o, pl.ds(4 * h, 4)])
    g2x = AllGather(rx, lambda o: loadT.at[2, o, z], lambda o, h: loadT.at[2, o, z, pl.ds(16 * h, 16)])
    g2z = AllGather(rz, lambda o: loadT.at[2, :, o], lambda o, h: loadT.at[2, :, o, pl.ds(16 * h, 16)])

    outs = []

    def use(v, q, first=False):
        block = loadT[v, q].reshape(256, 256).T
        stage[v, q] = block
        out = pltpu.make_async_copy(
            stage.at[v, q], loadings.at[v, pl.ds(pl.multiple_of(q * 256, 256), 256)], out_sems.at[len(outs)])
        out.start()
        outs.append(out)
        product = jnp.dot(feats[v, q], block.astype(BF16), preferred_element_type=F32)
        contrib[...] = product if first else contrib[...] + product

    g2x.step(1)
    gz.step(1)
    g2x.step(2)
    gz.step(2)
    g2x.final()
    g2z.step(1)
    gz.step(3)
    gz.step(4)
    gz.final()
    gx.step(1)
    g2z.step(2)
    use(0, x, True)
    use(1, x)
    g2z.step(3)
    gx.step(2)
    g2z.step(4)
    for d in (1, 3):
        for v in (0, 1):
            use(v, rx.at(d))
    g2z.final()
    for d in range(4):
        use(2, rx.at(d))
    gx.final()
    for v in (0, 1):
        use(v, rx.at(2))
    links.drain()
    for out in outs:
        out.wait()


def merge(contrib, merged, gram, mine_in, mine_sum, land_m, part, part_in, part_sum, land_g, over_x, over_z, total,
          send_sems, recv_sems):
    y, x, z, c = place()
    links = Links(send_sems, recv_sems)
    rx, rz, ry = rings(links, x, z, y)
    partner = {"col": 1 - c}
    greet([rx.device(-1), rx.device(1), rz.device(-1), rz.device(1), ry.device(-1), ry.device(1), partner])

    slot = links.slot()
    links.send(slot, contrib.at[1 - c], mine_in, partner)
    links.arrived(slot, mine_in, partner)
    mine_sum[...] = contrib[c] + mine_in[...]
    ms = ReduceScatter(ry, lambda o, h: mine_sum.at[o, pl.ds(64 * h, 64)], land_m)
    ms.step(1)
    ms.step(2)
    halves = ms.final()
    for h in (0, 1):
        merged[c, y, pl.ds(64 * h, 64)] = halves[h]
    rows = merged[c, y]
    part[...] = lax.dot_general(rows, rows, (((0,), (0,)), ((), ())), precision=HIGH,
                                preferred_element_type=F32).reshape(2, NY, 32, 256)
    slot = links.slot()
    links.send(slot, part.at[1 - c], part_in, partner)
    mg = AllGather(ry, lambda o: merged.at[c, o], lambda o, h: merged.at[c, o, pl.ds(64 * h, 64)])
    links.arrived(slot, part_in, partner)
    part_sum[...] = part[c] + part_in[...]
    gs = ReduceScatter(ry, lambda o, h: part_sum.at[o, pl.ds(16 * h, 16)], land_g)
    gs.step(1)
    gs.step(2)
    halves = gs.final()
    for h in (0, 1):
        over_x[x, pl.ds(16 * h, 16)] = halves[h]
    gx = AllGather(rx, lambda o: over_x.at[o], lambda o, h: over_x.at[o, pl.ds(16 * h, 16)])
    gx.step(1)
    mg.step(1)
    gx.step(2)
    gx.final()
    over_z[z] = (over_x[0] + over_x[1]) + (over_x[2] + over_x[3])
    gz = AllGather(rz, lambda o: over_z.at[o], lambda o, h: over_z.at[o, pl.ds(16 * h, 16)])
    gz.step(1)
    mg.step(2)
    gz.step(2)
    mg.final()
    slot = links.slot()
    links.send(slot, merged.at[c], merged.at[c], partner)
    gz.step(3)
    gz.step(4)
    gz.final()
    acc = over_z[0]
    for i in range(1, NZ):
        acc = acc + over_z[i]
    gram[c, y] = acc
    gy = AllGather(ry, lambda o: gram.at[c, o], lambda o, h: gram.at[c, o, pl.ds(16 * h, 16)])
    gy.step(1)
    gy.step(2)
    gy.final()
    last = links.slot()
    links.send(last, gram.at[c], gram.at[c], partner)
    links.arrived(slot, merged.at[1 - c], partner)
    links.arrived(last, gram.at[1 - c], partner)
    links.drain()


def shards(sketched, widths, inv_factor, shared):
    total_rows = shared.shape[0] * lax.axis_size("sent")
    vmem, smem, anywhere = (pl.BlockSpec(memory_space=m) for m in (pltpu.VMEM, pltpu.SMEM, pl.ANY))

    def buf(*shape):
        return pltpu.VMEM(shape, F32)

    sems = [pltpu.SemaphoreType.DMA((SEMS,)), pltpu.SemaphoreType.DMA((SEMS,))]

    def kernel_a(*refs):
        project(1.0 / math.sqrt(total_rows), *refs)

    loadings, contrib = pl.pallas_call(
        kernel_a,
        name="project",
        out_shape=(jax.ShapeDtypeStruct((3, 1024, 256), F32), jax.ShapeDtypeStruct((1024, 256), F32)),
        in_specs=[smem, vmem, vmem, anywhere],
        out_specs=(anywhere, vmem),
        scratch_shapes=[
            pltpu.VMEM((3, 4, 1024, 256), BF16), pltpu.VMEM((256, 1024), BF16),
            buf(3, 4, 8, 32, 256), buf(2, 2, 2, 2, 4, 32, 256), buf(2, 8, 32, 256), buf(2, 2, 2, 4, 16, 256),
            buf(2, 2, 4, 4, 16, 256), buf(4, 32, 256), buf(2, 2, 2, 16, 256), buf(8, 3, 32, 256),
            buf(3, 4, 64, 256), buf(2, 4, 3, 32, 256), buf(4, 3, 32, 256), buf(4, 3, 32, 256),
            buf(2, 2, 2, 3, 16, 256), buf(2, 4, 3, 32, 256), buf(8, 3, 32, 256), buf(2, 2, 4, 3, 16, 256),
            buf(3, 4, 8, 32, 256), buf(3, 4, 256, 256), *sems,
            pltpu.SemaphoreType.DMA((12,)), pltpu.SemaphoreType.DMA((12,)), pltpu.SemaphoreType.DMA],
        compiler_params=pltpu.CompilerParams(collective_id=0, has_side_effects=True, vmem_limit_bytes=56 * 2**20),
    )(widths, shared, inv_factor, sketched)

    merged, gram = pl.pallas_call(
        merge,
        name="merge",
        out_shape=(jax.ShapeDtypeStruct((2, NY, 128, 256), F32), jax.ShapeDtypeStruct((2, NY, 32, 256), F32)),
        in_specs=[vmem],
        out_specs=(vmem, vmem),
        scratch_shapes=[
            buf(4, 128, 256), buf(4, 128, 256), buf(2, 2, 2, 64, 256), buf(2, 4, 32, 256), buf(4, 32, 256),
            buf(4, 32, 256), buf(2, 2, 2, 16, 256), buf(4, 32, 256), buf(8, 32, 256), buf(2, 4, 32, 256), *sems],
        compiler_params=pltpu.CompilerParams(collective_id=1, has_side_effects=True, vmem_limit_bytes=32 * 2**20),
    )(contrib.reshape(2, NY, 128, 256))
    merged, gram = merged.reshape(1024, 256), gram.reshape(256, 256)
    lower = jnp.linalg.cholesky(gram)
    updated = lax.linalg.triangular_solve(
        lower, merged, left_side=False, lower=True, transpose_a=True
    ) * math.sqrt(total_rows)
    return (loadings, updated)


def solution(mesh):
    return jax.shard_map(
        shards,
        mesh=mesh,
        in_specs=(P("view", "sent", "col"), P("view"), P("view", "sent", "col"), P("sent", None)),
        out_specs=(P("view", "col", None), P("sent", None)),
        check_vma=False,
    )
```

time: 665 us -> 258 us (0.39)
  waiting for transfers between devices: 547 us -> 0 us
  Pallas kernels: 0 us -> 188 us
  matrix products: 29 us -> 2.7 us
  between operations: 15.2 us -> 2.07 us
    psum x5 -> x0, waiting for transfers between devices: 547 us -> none  [the longest x1 158 us: shards(): proj = lax.psum(terms, 'sent') * keep_cols]
    pallas_call x0 -> x2, Pallas kernels: none -> 188 us  [the longest x1 129 us: shards(): pl.pallas_call(kernel_a, name='project', out_shape=(jax.ShapeDtypeStruct(...]
    dot_general x5 -> x0, matrix products: 26.7 us -> none  [the longest x1 6.69 us: shards(): jnp.einsum('vrd,rk->vdk', sketched, shared, preferred_element_type=jnp.fl...]
  transfers between devices with their start and end apart: 5 -> 0, of which waited for: 5 -> 0; matrix products, arithmetic and copies ran while one was open for 1% -> 0% of each run, Pallas kernels for 0% -> 0%
where the time goes in v1:
time: 258 us; the launch traced here: 257 us
  Pallas kernels  188 us (73%)
  other arithmetic  54.2 us (21%)
  local copies, waits for them, and re-layouts  10.3 us (4%)
  matrix products  2.7 us (1%)
    pallas_call x1, Pallas kernels, shards(): pl.pallas_call(kernel_a, name='project', out_shape=(jax.ShapeDtypeStruct(...  129 us
    pallas_call x1, Pallas kernels, shards(): pl.pallas_call(merge, name='merge', out_shape=(jax.ShapeDtypeStruct((2, N...  59 us
    another operation x6, other arithmetic, shards(): lower = jnp.linalg.cholesky(gram)  34.1 us
    another operation x3, other arithmetic, shards(): lax.linalg.triangular_solve(lower, merged, left_side=False, lower=True, t...  19.9 us
    unnamed x4, local copies, waits for them, and re-layouts  6.28 us

profile of v1, /device:TPU:1, one launch (start us, length us, event | category | flops | bytes accessed | tf_op | source)
XLA Modules:
  0.0 257.4 jit_solution(8153138046631328841)
XLA Ops:
  0.6 129.2 %project.1 = (f32[3,1024,256]{2,1,0:T(8,128)}, f32[1024,256]{1,0:T(8,128)}) custom-call(s32[3]{0:T(128)} %refs_0_.1, bf16[1024,256]{1,0:T(8,128)(2,1)} %refs_1_.1, f32[3,64,1024]{2,1,0:T(8,128)} %refs_2_.1, bf16[3,1024,1024]{2,1,0:T(8,128)(2,1)} %refs_3_.1), custom_call_target="tpu_custom_call" | custom-call | tf_op jit(solution)/shard_map/project/pallas_call | solution.py:401
  129.8 0.0 copy-start
  129.8 1.2 copy-done
  131.0 59.0 %merge.1 = (f32[2,4,128,256]{3,2,1,0:T(8,128)S(1)}, f32[2,4,32,256]{3,2,1,0:T(8,128)S(1)}) custom-call(f32[2,4,128,256]{3,2,1,0:T(8,128)S(1)} %bitcast.38), custom_call_target="tpu_custom_call" | custom-call | tf_op jit(solution)/shard_map/merge/pallas_call | solution.py:418
  190.1 0.1 copy.9
  190.3 11.9 %cholesky.50 = f32[128,128]{1,0:T(8,128)S(1)} custom-call(f32[128,128]{1,0:T(8,128)S(1)} %cholesky.118), custom_call_target="Cholesky" | custom-call | tf_op jit(solution)/shard_map/jit(cholesky)/cholesky | solution.py:430
  202.2 9.8 %custom-call.14 = f32[1,128,128]{1,2,0:T(8,128)S(1)} custom-call(f32[1,128,128]{2,1,0:T(8,128)S(1)} %get-tuple-element.35), custom_call_target="InvertDiagBlocksLowerTriangular" | custom-call | tf_op jit(solution)/shard_map/jit(cholesky)/cholesky | solution.py:430
  212.0 0.2 constant_dynamic-update-slice_fusion.1
  212.2 0.3 convolution_subtract_fusion.1
  212.5 11.7 %cholesky.105 = f32[128,128]{1,0:T(8,128)S(1)} custom-call(f32[128,128]{1,0:T(8,128)S(1)} %convolution_subtract_fusion.1), custom_call_target="Cholesky" | custom-call | tf_op jit(solution)/shard_map/jit(cholesky)/cholesky | solution.py:430
  224.2 0.6 compare_reduce_fusion
  226.3 0.1 triangular_solve.58
  226.3 3.8 %while.1 = (s32[]{:T(128)}, f32[256,256]{1,0:T(8,128)S(1)}, s32[2,2]{1,0:T(2,128)S(1)}, f32[2,128,128]{2,1,0:T(8,128)S(1)}, s32[]{:T(128)}) while((s32[]{:T(128)}, f32[256,256]{1,0:T(8,128)S(1)}, s32[2,2]{1,0:T(2,128)S(1)}, f32[2,128,128]{2,1,0:T(8,128)S(1)}, s32[]{:T(128)}) %tuple.29), condition=%wide.while_cond, body=%wide.while_body.sunk | while | flops 2 | bytes 131181 | solution.py:431
  226.3 0.6 fusion.14
  226.9 1.3 bitcast_dynamic-update-slice_fusion.2
  228.2 0.6 fusion.14
  228.8 1.3 bitcast_dynamic-update-slice_fusion.2
  230.1 19.9 %custom-call.15 = f32[2,128,128]{1,2,0:T(8,128)S(1)} custom-call(f32[2,128,128]{2,1,0:T(8,128)S(1)} %get-tuple-element.17), custom_call_target="InvertDiagBlocksLowerTriangular" | custom-call | tf_op jit(solution)/shard_map/triangular_solve | solution.py:431
  250.0 0.6 fusion
  250.6 1.0 convolution_subtract_fusion
  251.6 0.6 fusion.3
  252.3 0.1 maximum_multiply_fusion
  252.4 1.3 copy.10
  253.7 3.8 %copy.23 = f32[3,1024,256]{2,1,0:T(8,128)} copy(f32[3,1024,256]{2,1,0:T(8,128)} %get-tuple-element.86) | data formatting | bytes 6291456
  (10 shorter events, 0.2 us)
Async XLA Ops:
  129.8 1.2 copy-start

commit v2 on v1

--- a/solution.py
+++ b/solution.py
@@ -386,6 +386,82 @@
     links.drain()
 
 
+PANEL = 32
+
+
+def panel_inverse(tiles, lane0):
+    groups = PANEL // 8
+    sub = lax.broadcasted_iota(jnp.int32, (8, 128), 0)
+    lane = lax.broadcasted_iota(jnp.int32, (8, 128), 1)
+
+    def spread(tile, s):
+        return jnp.broadcast_to(tile[s:s + 1, :], (8, 128))
+
+    cols = [{g: jnp.broadcast_to(tiles[g][:, lane0 + j:lane0 + j + 1], (8, 128)) for g in range(j // 8, groups)}
+            for j in range(PANEL)]
+    unit = [jnp.where(lane == sub + 8 * g, 1.0, 0.0).astype(F32) for g in range(groups)]
+    pivots = [jnp.ones((8, 128), F32) for g in range(groups)]
+    for k in range(PANEL):
+        gk, sk = divmod(k, 8)
+        pivot = spread(cols[k][gk], sk)
+        inverse = 1.0 / pivot
+        pivots[gk] = jnp.where(sub == sk, pivot, pivots[gk])
+        mult = {g: cols[k][g] * inverse for g in range(gk, groups)}
+        for j in range(k + 1, PANEL):
+            gj, sj = divmod(j, 8)
+            entry = spread(cols[k][gj], sj)
+            for g in range(gj, groups):
+                cols[j][g] = cols[j][g] - mult[g] * entry
+        row = spread(unit[gk], sk)
+        for g in range(gk, groups):
+            m = jnp.where(sub > sk, mult[g], 0.0) if g == gk else mult[g]
+            unit[g] = unit[g] - m * row
+    return jnp.concatenate([unit[g] * lax.rsqrt(pivots[g]) for g in range(groups)], axis=0)[:, :PANEL]
+
+
+def tn(a, b):
+    return lax.dot_general(a, b, (((0,), (0,)), ((), ())), precision=HIGH, preferred_element_type=F32)
+
+
+def factor_inverse(work, inverse, between):
+    n = work.shape[0]
+    for p in range(n // PANEL):
+        r0 = p * PANEL
+        lt = r0 // 128 * 128
+        tiles = [work[r0 + 8 * g:r0 + 8 * g + 8, lt:lt + 128] for g in range(PANEL // 8)]
+        block = panel_inverse(tiles, r0 - lt)
+        col = lax.broadcasted_iota(jnp.int32, (PANEL, n), 1)
+        row = lax.broadcasted_iota(jnp.int32, (PANEL, n), 0)
+        here = (col >= r0) & (col < r0 + PANEL)
+        wide = jnp.where(here, jnp.where(col == row + r0, 1.0, 0.0), work[r0:r0 + PANEL, :])
+        u = nn(block, wide)
+        inverse[r0:r0 + PANEL, :] = jnp.where(col < r0 + PANEL, u, 0.0)
+        between(p)
+        r1 = r0 + PANEL
+        if r1 < n:
+            base = r1 // 128 * 128
+            upd = tn(u[:, base:], u)[r1 - base:]
+            col = lax.broadcasted_iota(jnp.int32, (n - r1, n), 1)
+            here = (col >= r0) & (col < r1)
+            work[r1:, :] = jnp.where(here, 0.0, work[r1:, :]) - upd
+
+
+def solve(root, gram, merged, loaded, updated, loadings, work, inverse, passing, in_sem, out_sem):
+    bring = pltpu.make_async_copy(loaded, passing, in_sem)
+    put = pltpu.make_async_copy(passing, loadings, out_sem)
+    bring.start()
+    work[...] = gram[...]
+
+    def between(panel):
+        if panel == 2:
+            bring.wait()
+            put.start()
+
+    factor_inverse(work, inverse, between)
+    updated[...] = nt(merged[...], inverse[...]) * root
+    put.wait()
+
+
 def shards(sketched, widths, inv_factor, shared):
     total_rows = shared.shape[0] * lax.axis_size("sent")
     vmem, smem, anywhere = (pl.BlockSpec(memory_space=m) for m in (pltpu.VMEM, pltpu.SMEM, pl.ANY))
@@ -427,10 +503,20 @@
         compiler_params=pltpu.CompilerParams(collective_id=1, has_side_effects=True, vmem_limit_bytes=32 * 2**20),
     )(contrib.reshape(2, NY, 128, 256))
     merged, gram = merged.reshape(1024, 256), gram.reshape(256, 256)
-    lower = jnp.linalg.cholesky(gram)
-    updated = lax.linalg.triangular_solve(
-        lower, merged, left_side=False, lower=True, transpose_a=True
-    ) * math.sqrt(total_rows)
+
+    def kernel_c(*refs):
+        solve(math.sqrt(total_rows), *refs)
+
+    updated, loadings = pl.pallas_call(
+        kernel_c,
+        name="solve",
+        out_shape=(jax.ShapeDtypeStruct((1024, 256), F32), jax.ShapeDtypeStruct((3, 1024, 256), F32)),
+        in_specs=[vmem, vmem, anywhere],
+        out_specs=(vmem, anywhere),
+        scratch_shapes=[buf(256, 256), buf(256, 256), buf(3, 1024, 256),
+                        pltpu.SemaphoreType.DMA, pltpu.SemaphoreType.DMA],
+        compiler_params=pltpu.CompilerParams(vmem_limit_bytes=32 * 2**20),
+    )(gram, merged, loadings)
     return (loadings, updated)
 
 

time: 258 us -> 205 us (0.79)
  other arithmetic: 54.2 us -> 0 us
  Pallas kernels: 188 us -> 201 us
  local copies, waits for them, and re-layouts: 10.3 us -> 3.1 us
  matrix products: 2.7 us -> 0 us
    another operation x9 -> x0, other arithmetic: 54 us -> none  [the longest x6 34.1 us: shards(): lower = jnp.linalg.cholesky(gram)]
    pallas_call x0 -> x1, Pallas kernels: none -> 12.5 us  [shards(): pl.pallas_call(kernel_c, name='solve', out_shape=(jax.ShapeDtypeStruct((1...]
    another operation x9 -> x0, local copies, waits for them, and re-layouts: 3.84 us -> none
    unnamed x4, local copies, waits for them, and re-layouts: 6.28 us -> 3.1 us
    another operation x5 -> x0, matrix products: 2.7 us -> none  [the longest x3 2.23 us: shards(): lax.linalg.triangular_solve(lower, merged, left_side=False, lower=True, t...]
where the time goes in v2:
time: 205 us
  Pallas kernels  201 us (98%)
  local copies, waits for them, and re-layouts  3.1 us (2%)
    pallas_call x1, Pallas kernels, shards(): pl.pallas_call(kernel_a, name='project', out_shape=(jax.ShapeDtypeStruct(...  129 us
    pallas_call x1, Pallas kernels, shards(): pl.pallas_call(merge, name='merge', out_shape=(jax.ShapeDtypeStruct((2, N...  59 us
    pallas_call x1, Pallas kernels, shards(): pl.pallas_call(kernel_c, name='solve', out_shape=(jax.ShapeDtypeStruct((1...  12.5 us

profile of v2, /device:TPU:1, one launch (start us, length us, event | category | flops | bytes accessed | tf_op | source)
XLA Modules:
  0.0 204.7 jit_solution(9789589432503271565)
XLA Ops:
  0.6 129.2 %project.1 = (f32[3,1024,256]{2,1,0:T(8,128)}, f32[1024,256]{1,0:T(8,128)}) custom-call(s32[3]{0:T(128)} %refs_0_.1, bf16[1024,256]{1,0:T(8,128)(2,1)} %refs_1_.1, f32[3,64,1024]{2,1,0:T(8,128)} %refs_2_.1, bf16[3,1024,1024]{2,1,0:T(8,128)(2,1)} %refs_3_.1), custom_call_target="tpu_custom_call" | custom-call | tf_op jit(solution)/shard_map/project/pallas_call | solution.py:477
  129.8 0.0 copy-start.1
  129.8 1.2 copy-done.1
  131.0 59.0 %merge.1 = (f32[2,4,128,256]{3,2,1,0:T(8,128)S(1)}, f32[2,4,32,256]{3,2,1,0:T(8,128)S(1)}) custom-call(f32[2,4,128,256]{3,2,1,0:T(8,128)S(1)} %bitcast.4), custom_call_target="tpu_custom_call" | custom-call | tf_op jit(solution)/shard_map/merge/pallas_call | solution.py:494
  190.1 0.0 copy-start
  190.1 1.9 copy-done
  192.0 12.5 %solve.1 = (f32[1024,256]{1,0:T(8,128)}, f32[3,1024,256]{2,1,0:T(8,128)}) custom-call(f32[256,256]{1,0:T(8,128)S(1)} %bitcast.5, f32[1024,256]{1,0:T(8,128)S(1)} %bitcast.3, f32[3,1024,256]{2,1,0:T(8,128)S(1)} %copy-done), custom_call_target="tpu_custom_call" | custom-call | tf_op jit(solution)/shard_map/solve/pallas_call | solution.py:510
Async XLA Ops:
  129.8 1.2 copy-start.1
  190.1 1.9 copy-start

commit v3 on v2

v3 whole, which is shorter than its diff:
```python
import math

import jax
import jax.numpy as jnp
from jax import lax
from jax.experimental import pallas as pl
from jax.experimental.pallas import tpu as pltpu
from jax.sharding import PartitionSpec as P

MESH = pl.DeviceIdType.MESH
HIGH = lax.Precision.HIGHEST
F32 = jnp.float32
BF16 = jnp.bfloat16
NX, NZ, NY = 4, 8, 4
SEMS = 256


class Clock:
    def __init__(self):
        self.now, self.busy, self.flows = 0.0, {}, []

    def sent(self, axis, kib):
        rate = 0.0068 if axis == "c" else 0.022
        self.busy[axis] = max(self.now, self.busy.get(axis, 0.0)) + kib * rate
        return self.busy[axis] + (1.0 if axis == "c" else 1.8)

    def add(self, start, flow):
        self.flows.append([start, len(self.flows), flow])

    def run(self):
        while self.flows:
            item = min(self.flows)
            self.now = max(self.now, item[0]) + 0.1
            try:
                item[0] = next(item[2])
            except StopIteration:
                self.flows.remove(item)


class Links:
    def __init__(self, send_sems, recv_sems):
        self.send_sems, self.recv_sems, self.used, self.sent = send_sems, recv_sems, 0, []
        self.clock = Clock()

    def slot(self):
        self.used += 1
        assert self.used <= SEMS
        return self.used - 1

    def copy(self, slot, src, dst, device):
        return pltpu.make_async_remote_copy(
            src_ref=src, dst_ref=dst, send_sem=self.send_sems.at[slot], recv_sem=self.recv_sems.at[slot],
            device_id=device, device_id_type=MESH)

    def send(self, slot, src, dst, device):
        made = self.copy(slot, src, dst, device)
        made.start()
        self.sent.append(made)

    def arrived(self, slot, dst, device):
        self.copy(slot, dst, dst, device).wait_recv()

    def drain(self):
        for made in self.sent:
            made.wait_send()
        self.sent = []


class Ring:
    def __init__(self, links, axis, size, pos, device):
        self.links, self.axis, self.size, self.pos, self.device = links, axis, size, pos, device

    def at(self, delta):
        return lax.rem(self.pos + (delta % self.size), self.size)


class ReduceScatter:
    def __init__(self, ring, own, landing, kib):
        self.ring, self.own, self.landing, self.kib = ring, own, landing, kib
        self.half_ring = ring.size // 2
        self.slots = {(d, kind, t): ring.links.slot()
                      for t in range(1, self.half_ring + 1) for d in (0, 1) for kind in (0, 1)
                      if not (kind == 1 and t == self.half_ring)}

    def wait(self, d, kind, t):
        sign = (-1, 1)[d]
        buf = self.landing.at[d, kind, t - 1]
        self.ring.links.arrived(self.slots[d, kind, t], buf, self.ring.device(sign))
        return buf

    def step(self, t, kind):
        for d, sign in ((0, -1), (1, 1)):
            dist = self.half_ring + 1 - t - kind
            mine = self.own(self.ring.at(sign * dist), d if kind == 0 else 1 - d)
            if t == 1:
                src = mine
            else:
                src = self.wait(d, kind, t - 1)
                src[...] = src[...] + mine[...]
            self.ring.links.send(self.slots[d, kind, t], src, self.landing.at[d, kind, t - 1],
                                 self.ring.device(sign))
        return self.ring.links.clock.sent(self.ring.axis, self.kib)

    def flow(self):
        due = {}
        for t in range(1, self.half_ring + 1):
            for kind in (0, 1):
                if (0, kind, t) not in self.slots:
                    continue
                if t > 1:
                    yield due[kind]
                due[kind] = self.step(t, kind)
        yield max(due.values())
        last = self.half_ring
        out = []
        for h in (0, 1):
            far = self.wait(h, 0, last)
            near = self.wait(1 - h, 1, last - 1)
            out.append(self.own(self.ring.pos, h)[...] + far[...] + near[...])
        return out


class AllGather:
    def __init__(self, ring, full, half, kib):
        self.ring, self.full, self.half, self.kib = ring, full, half, kib
        self.half_ring = ring.size // 2
        self.slots = {(d, t): ring.links.slot() for t in range(1, self.half_ring + 1) for d in (0, 1)}

    def view(self, d, t, owner):
        return self.half(owner, d) if t == self.half_ring else self.full(owner)

    def wait(self, d, t):
        sign = (-1, 1)[d]
        dst = self.view(d, t, self.ring.at(-sign * t))
        self.ring.links.arrived(self.slots[d, t], dst, self.ring.device(sign))

    def step(self, t):
        for d, sign in ((0, -1), (1, 1)):
            if t > 1:
                self.wait(d, t - 1)
            src = self.view(d, t, self.ring.at(-sign * (t - 1)))
            self.ring.links.send(self.slots[d, t], src, src, self.ring.device(sign))
        return self.ring.links.clock.sent(self.ring.axis, self.kib if t < self.half_ring else self.kib / 2)

    def final(self):
        for d in (0, 1):
            self.wait(d, self.half_ring)

    def flow(self, reached=None):
        for t in range(1, self.half_ring + 1):
            due = self.step(t)
            if reached is not None:
                reached(t - 1)
            yield due
        self.final()
        if reached is not None:
            reached(self.half_ring)


class Direct:
    def __init__(self, ring, source, target):
        self.ring, self.target = ring, target
        order = sorted(range(1, ring.size), key=lambda d: -min(d, ring.size - d))
        self.slots = {d: ring.links.slot() for d in order}
        for d in order:
            ring.links.send(self.slots[d], source(ring.at(d)), target(ring.pos), ring.device(d))

    def final(self):
        for d, slot in self.slots.items():
            self.ring.links.arrived(slot, self.target(self.ring.at(-d)), self.ring.device(d))


def place():
    y, s, c = lax.axis_index("view"), lax.axis_index("sent"), lax.axis_index("col")
    return y, s // NZ, lax.rem(s, NZ), c


def rings(links, x, z, y):
    def x_dev(delta):
        return {"sent": lax.rem(x + (delta % NX), NX) * NZ + z}

    def z_dev(delta):
        return {"sent": x * NZ + lax.rem(z + (delta % NZ), NZ)}

    def y_dev(delta):
        return {"view": lax.rem(y + (delta % NY), NY)}

    return (Ring(links, "x", NX, x, x_dev), Ring(links, "z", NZ, z, z_dev), Ring(links, "y", NY, y, y_dev))


def nt(a, b):
    return lax.dot_general(a, b, (((1,), (1,)), ((), ())), precision=HIGH, preferred_element_type=F32)


def nn(a, b):
    return lax.dot_general(a, b, (((1,), (0,)), ((), ())), precision=HIGH, preferred_element_type=F32)


def project(scale, widths, shared, inv, sketched, loadings, merged, gram,
            feats, sharedT, terms, land_x, quarter, land_z, land_z2, quarter2, land_x2, proj, invx,
            part, part_in, part_sum, land_h, half, back, land_b, loadT, stage,
            contrib, mine_in, mine_sum, land_m, outer, outer_in, outer_sum, from_y, over_x, over_z,
            send_sems, recv_sems, feat_sems, out_sems, own_sem):
    y, x, z, c = place()
    links = Links(send_sems, recv_sems)
    clock = links.clock
    rx, rz, ry = rings(links, x, z, y)
    partner = {"col": 1 - c}

    barrier = pltpu.get_barrier_semaphore()
    peers = [partner] + [ring.device(d) for ring in (rx, rz, ry) for d in range(1, ring.size)]
    for peer in peers:
        pl.semaphore_signal(barrier, inc=1, device_id=peer, device_id_type=MESH)

    quarters = [rx.at(d) for d in (2, 3, 1, 0)]
    loads = {}
    for i, v in enumerate((2, 0, 1)):
        for n, q in enumerate(quarters):
            loads[v, n] = pltpu.make_async_copy(
                sketched.at[v, :, pl.ds(pl.multiple_of(q * 256, 256), 256)], feats.at[v, q],
                feat_sems.at[4 * i + n])
            loads[v, n].start()
    own_inv = pltpu.make_async_copy(
        inv.at[:, :, pl.ds(pl.multiple_of(x * 256, 256), 256)], invx.at[:, x], own_sem)
    own_inv.start()
    sharedT[...] = shared[...].T

    first_col = c * 1024 + x * 256
    lane = lax.broadcasted_iota(jnp.int32, (16, 256), 1)
    row = (lane // 64) * (64 * NZ) + z * 64 + lax.rem(lane, 64)

    def lanes_kept(v, value):
        return jnp.where(first_col + lane < widths[v], value, 0.0)

    inv_slots = {}

    def send_inv():
        for d in (1, 3, 2):
            inv_slots[d] = links.slot()
            links.send(inv_slots[d], inv.at[:, :, pl.ds(pl.multiple_of(rx.at(d) * 256, 256), 256)],
                       invx.at[:, x], rx.device(d))
        clock.sent("x", 288)
        yield clock.now

    def need_inv():
        if None not in inv_slots:
            own_inv.wait()
            for d in (1, 3, 2):
                links.arrived(inv_slots[d], invx.at[:, rx.at(-d)], rx.device(d))
            inv_slots[None] = None

    def swap(src, dst, landed):
        slot = links.slot()
        links.send(slot, src, dst, partner)
        yield clock.sent("c", 128)
        links.arrived(slot, landed, partner)

    outs = []

    def use(v, q):
        block = loadT[v, q].reshape(256, 256).T
        stage[v, q] = block
        out = pltpu.make_async_copy(
            stage.at[v, q], loadings.at[v, pl.ds(pl.multiple_of(q * 256, 256), 256)], out_sems.at[len(outs)])
        out.start()
        product = jnp.dot(feats[v, q], block.astype(BF16), preferred_element_type=F32).reshape(2, NY, 128, 256)
        contrib[...] = contrib[...] + product if outs else product
        outs.append(out)

    def reached_x(v, t):
        for d in sorted({t % NX, -t % NX}):
            use(v, rx.at(d))

    def view_flow(v):
        for n, q in enumerate(quarters):
            loads[v, n].wait()
            terms[v, q] = jnp.dot(sharedT[...], feats[v, q], preferred_element_type=F32).reshape(NZ, 32, 256)
        if v == 2:
            pl.semaphore_wait(barrier, len(peers))
            halves = yield from ReduceScatter(
                rz, lambda o, h: terms.at[2, :, o, pl.ds(16 * h, 16)], land_z2, 64).flow()
            for h in (0, 1):
                quarter2[:, pl.ds(16 * h, 16)] = halves[h]
            halves = yield from ReduceScatter(rx, lambda o, h: quarter2.at[o, pl.ds(16 * h, 16)], land_x2, 16).flow()
        else:
            halves = yield from ReduceScatter(
                rx, lambda o, h: terms.at[v, o, pl.ds(4 * h, 4)], land_x.at[v], 128).flow()
            for h in (0, 1):
                quarter[v, pl.ds(4 * h, 4)] = halves[h]
            halves = yield from ReduceScatter(
                rz, lambda o, h: quarter.at[v, o, pl.ds(16 * h, 16)], land_z.at[v], 16).flow()
        for h in (0, 1):
            proj[v, z, pl.ds(16 * h, 16)] = lanes_kept(v, halves[h] * scale)
        yield from AllGather(rz, lambda o: proj.at[v, o], lambda o, h: proj.at[v, o, pl.ds(16 * h, 16)], 32).flow()

        need_inv()
        part[v] = nt(proj[v].reshape(256, 256), invx[v].reshape(256, 256)).reshape(2, NX, 32, 256)
        yield from swap(part.at[v, 1 - c], part_in.at[v], part_in.at[v])
        part_sum[v] = part[v, c] + part_in[v]
        halves = yield from ReduceScatter(
            rx, lambda o, h: part_sum.at[v, o, pl.ds(16 * h, 16)], land_h.at[v], 16).flow()
        for h in (0, 1):
            half[v, c, x, pl.ds(16 * h, 16)] = jnp.where(row < widths[v], halves[h], 0.0)
        yield from AllGather(rx, lambda o: half.at[v, c, o], lambda o, h: half.at[v, c, o, pl.ds(16 * h, 16)], 32).flow()
        yield from swap(half.at[v, c], half.at[v, c], half.at[v, 1 - c])

        back[v] = nn(half[v].reshape(256, 256), invx[v].reshape(256, 256)).reshape(NZ, 32, 256)
        halves = yield from ReduceScatter(
            rz, lambda o, h: back.at[v, o, pl.ds(16 * h, 16)], land_b.at[v], 16).flow()
        for h in (0, 1):
            loadT[v, x, z, pl.ds(16 * h, 16)] = lanes_kept(v, halves[h])
        if v == 2:
            yield from AllGather(rx, lambda o: loadT.at[2, o, z], lambda o, h: loadT.at[2, o, z, pl.ds(16 * h, 16)], 32).flow()
            yield from AllGather(rz, lambda o: loadT.at[2, :, o], lambda o, h: loadT.at[2, :, o, pl.ds(16 * h, 16)], 128).flow()
            for q in range(NX):
                use(2, q)
        else:
            yield from AllGather(rz, lambda o: loadT.at[v, x, o], lambda o, h: loadT.at[v, x, o, pl.ds(16 * h, 16)], 32).flow()
            yield from AllGather(
                rx, lambda o: loadT.at[v, o], lambda o, h: loadT.at[v, o, pl.ds(4 * h, 4)], 256,
            ).flow(lambda t: reached_x(v, t))

    clock.add(0.0, view_flow(2))
    clock.add(0.5, view_flow(0))
    clock.add(5.5, view_flow(1))
    clock.add(16.0, send_inv())
    clock.run()

    def now(flow):
        try:
            while True:
                next(flow)
        except StopIteration as stop:
            return stop.value

    now(swap(contrib.at[1 - c], mine_in, mine_in))
    mine_sum[...] = contrib[c] + mine_in[...]
    halves = now(ReduceScatter(ry, lambda o, h: mine_sum.at[o, pl.ds(64 * h, 64)], land_m, 64).flow())
    for h in (0, 1):
        merged[c, y, pl.ds(64 * h, 64)] = halves[h]
    rows = merged[c, y]
    outer[...] = tn(rows, rows).reshape(2, NY, 32, 256)
    now(swap(outer.at[1 - c], outer_in, outer_in))
    outer_sum[...] = outer[c] + outer_in[...]
    gs = Direct(ry, lambda o: outer_sum.at[o], lambda o: from_y.at[o])
    mg = AllGather(ry, lambda o: merged.at[c, o], lambda o, h: merged.at[c, o, pl.ds(64 * h, 64)], 128)
    from_y[y] = outer_sum[y]
    gs.final()
    mg.step(1)
    over_x[x] = (from_y[0] + from_y[1]) + (from_y[2] + from_y[3])
    Direct(rx, lambda o: over_x.at[x], lambda o: over_x.at[o]).final()
    over_z[z] = (over_x[0] + over_x[1]) + (over_x[2] + over_x[3])
    gz = Direct(rz, lambda o: over_z.at[z], lambda o: over_z.at[o])
    mg.step(2)
    mg.final()
    slot = links.slot()
    links.send(slot, merged.at[c], merged.at[c], partner)
    gz.final()
    acc = over_z[0]
    for i in range(1, NZ):
        acc = acc + over_z[i]
    gram[c, y] = acc
    Direct(ry, lambda o: gram.at[c, y], lambda o: gram.at[c, o]).final()
    now(swap(gram.at[c], gram.at[c], gram.at[1 - c]))
    links.arrived(slot, merged.at[1 - c], partner)
    links.drain()
    for out in outs:
        out.wait()


PANEL = 32


def panel_inverse(tiles, lane0):
    groups = PANEL // 8
    sub = lax.broadcasted_iota(jnp.int32, (8, 128), 0)
    lane = lax.broadcasted_iota(jnp.int32, (8, 128), 1)

    def spread(tile, s):
        return jnp.broadcast_to(tile[s:s + 1, :], (8, 128))

    cols = [{g: jnp.broadcast_to(tiles[g][:, lane0 + j:lane0 + j + 1], (8, 128)) for g in range(j // 8, groups)}
            for j in range(PANEL)]
    unit = [jnp.where(lane == sub + 8 * g, 1.0, 0.0).astype(F32) for g in range(groups)]
    pivots = [jnp.ones((8, 128), F32) for g in range(groups)]
    for k in range(PANEL):
        gk, sk = divmod(k, 8)
        pivot = spread(cols[k][gk], sk)
        inverse = 1.0 / pivot
        pivots[gk] = jnp.where(sub == sk, pivot, pivots[gk])
        mult = {g: cols[k][g] * inverse for g in range(gk, groups)}
        for j in range(k + 1, PANEL):
            gj, sj = divmod(j, 8)
            entry = spread(cols[k][gj], sj)
            for g in range(gj, groups):
                cols[j][g] = cols[j][g] - mult[g] * entry
        row = spread(unit[gk], sk)
        for g in range(gk, groups):
            m = jnp.where(sub > sk, mult[g], 0.0) if g == gk else mult[g]
            unit[g] = unit[g] - m * row
    return jnp.concatenate([unit[g] * lax.rsqrt(pivots[g]) for g in range(groups)], axis=0)[:, :PANEL]


def tn(a, b):
    return lax.dot_general(a, b, (((0,), (0,)), ((), ())), precision=HIGH, preferred_element_type=F32)


def factor_inverse(work, inverse, between):
    n = work.shape[0]
    for p in range(n // PANEL):
        r0 = p * PANEL
        lt = r0 // 128 * 128
        tiles = [work[r0 + 8 * g:r0 + 8 * g + 8, lt:lt + 128] for g in range(PANEL // 8)]
        block = panel_inverse(tiles, r0 - lt)
        col = lax.broadcasted_iota(jnp.int32, (PANEL, n), 1)
        row = lax.broadcasted_iota(jnp.int32, (PANEL, n), 0)
        here = (col >= r0) & (col < r0 + PANEL)
        wide = jnp.where(here, jnp.where(col == row + r0, 1.0, 0.0), work[r0:r0 + PANEL, :])
        u = nn(block, wide)
        inverse[r0:r0 + PANEL, :] = jnp.where(col < r0 + PANEL, u, 0.0)
        between(p)
        r1 = r0 + PANEL
        if r1 < n:
            base = r1 // 128 * 128
            upd = tn(u[:, base:], u)[r1 - base:]
            col = lax.broadcasted_iota(jnp.int32, (n - r1, n), 1)
            here = (col >= r0) & (col < r1)
            work[r1:, :] = jnp.where(here, 0.0, work[r1:, :]) - upd


def solve(root, gram, merged, loaded, updated, loadings, work, inverse, passing, in_sem, out_sem):
    bring = pltpu.make_async_copy(loaded, passing, in_sem)
    put = pltpu.make_async_copy(passing, loadings, out_sem)
    bring.start()
    work[...] = gram[...]

    def between(panel):
        if panel == 2:
            bring.wait()
            put.start()

    factor_inverse(work, inverse, between)
    updated[...] = nt(merged[...], inverse[...]) * root
    put.wait()


def shards(sketched, widths, inv_factor, shared):
    total_rows = shared.shape[0] * lax.axis_size("sent")
    vmem, smem, anywhere = (pl.BlockSpec(memory_space=m) for m in (pltpu.VMEM, pltpu.SMEM, pl.ANY))

    def buf(*shape):
        return pltpu.VMEM(shape, F32)

    sems = [pltpu.SemaphoreType.DMA((SEMS,)), pltpu.SemaphoreType.DMA((SEMS,))]

    def kernel_a(*refs):
        project(1.0 / math.sqrt(total_rows), *refs)

    loadings, merged, gram = pl.pallas_call(
        kernel_a,
        name="project",
        out_shape=(jax.ShapeDtypeStruct((3, 1024, 256), F32), jax.ShapeDtypeStruct((2, NY, 128, 256), F32),
                   jax.ShapeDtypeStruct((2, NY, 32, 256), F32)),
        in_specs=[smem, vmem, vmem, anywhere],
        out_specs=(anywhere, vmem, vmem),
        scratch_shapes=[
            pltpu.VMEM((3, 4, 1024, 256), BF16), pltpu.VMEM((256, 1024), BF16),
            buf(3, 4, 8, 32, 256), buf(2, 2, 2, 2, 4, 32, 256), buf(2, 8, 32, 256), buf(2, 2, 2, 4, 16, 256),
            buf(2, 2, 4, 4, 16, 256), buf(4, 32, 256), buf(2, 2, 2, 16, 256), buf(3, 8, 32, 256),
            buf(3, 4, 64, 256), buf(3, 2, 4, 32, 256), buf(3, 4, 32, 256), buf(3, 4, 32, 256),
            buf(3, 2, 2, 2, 16, 256), buf(3, 2, 4, 32, 256), buf(3, 8, 32, 256), buf(3, 2, 2, 4, 16, 256),
            buf(3, 4, 8, 32, 256), buf(3, 4, 256, 256),
            buf(2, 4, 128, 256), buf(4, 128, 256), buf(4, 128, 256), buf(2, 2, 2, 64, 256), buf(2, 4, 32, 256),
            buf(4, 32, 256), buf(4, 32, 256), buf(4, 32, 256), buf(4, 32, 256), buf(8, 32, 256), *sems,
            pltpu.SemaphoreType.DMA((12,)), pltpu.SemaphoreType.DMA((12,)), pltpu.SemaphoreType.DMA],
        compiler_params=pltpu.CompilerParams(collective_id=0, has_side_effects=True, vmem_limit_bytes=56 * 2**20),
    )(widths, shared, inv_factor, sketched)
    merged, gram = merged.reshape(1024, 256), gram.reshape(256, 256)

    def kernel_c(*refs):
        solve(math.sqrt(total_rows), *refs)

    updated, loadings = pl.pallas_call(
        kernel_c,
        name="solve",
        out_shape=(jax.ShapeDtypeStruct((1024, 256), F32), jax.ShapeDtypeStruct((3, 1024, 256), F32)),
        in_specs=[vmem, vmem, anywhere],
        out_specs=(vmem, anywhere),
        scratch_shapes=[buf(256, 256), buf(256, 256), buf(3, 1024, 256),
                        pltpu.SemaphoreType.DMA, pltpu.SemaphoreType.DMA],
        compiler_params=pltpu.CompilerParams(vmem_limit_bytes=32 * 2**20),
    )(gram, merged, loadings)
    return (loadings, updated)


def solution(mesh):
    return jax.shard_map(
        shards,
        mesh=mesh,
        in_specs=(P("view", "sent", "col"), P("view"), P("view", "sent", "col"), P("sent", None)),
        out_specs=(P("view", "col", None), P("sent", None)),
        check_vma=False,
    )
```

time: 205 us -> 174 us (0.85)
  Pallas kernels: 201 us -> 169 us
    pallas_call x1 -> x0, Pallas kernels: 59 us -> none  [shards(): pl.pallas_call(merge, name='merge', out_shape=(jax.ShapeDtypeStruct((2, N...]
    pallas_call x1, Pallas kernels: 129 us -> 157 us  [shards(): pl.pallas_call(kernel_a, name='project', out_shape=(jax.ShapeDtypeStruct(...]
where the time goes in v3:
time: 174 us
  Pallas kernels  169 us (97%)
  local copies, waits for them, and re-layouts  4.06 us (2%)
    pallas_call x1, Pallas kernels, shards(): pl.pallas_call(kernel_a, name='project', out_shape=(jax.ShapeDtypeStruct(...  157 us
    pallas_call x1, Pallas kernels, shards(): pl.pallas_call(kernel_c, name='solve', out_shape=(jax.ShapeDtypeStruct((1...  12.5 us
    unnamed x6, local copies, waits for them, and re-layouts  4.06 us

profile of v3, /device:TPU:1, one launch (start us, length us, event | category | flops | bytes accessed | tf_op | source)
XLA Modules:
  0.0 174.0 jit_solution(8815084115125213827)
XLA Ops:
  0.6 156.6 %project.1 = (f32[3,1024,256]{2,1,0:T(8,128)}, f32[2,4,128,256]{3,2,1,0:T(8,128)}, f32[2,4,32,256]{3,2,1,0:T(8,128)}) custom-call(s32[3]{0:T(128)} %refs_0_.1, bf16[1024,256]{1,0:T(8,128)(2,1)} %refs_1_.1, f32[3,64,1024]{2,1,0:T(8,128)} %refs_2_.1, bf16[3,1024,1024]{2,1,0:T(8,128)(2,1)} %refs_3_.1), custom_call_target="tpu_custom_call" | custom-call | tf_op jit(solution)/shard_map/project/pallas_call | solution.py:459
  157.3 0.0 copy-start
  157.3 1.9 %copy-done = f32[3,1024,256]{2,1,0:T(8,128)S(1)} copy-done((f32[3,1024,256]{2,1,0:T(8,128)S(1)}, f32[3,1024,256]{2,1,0:T(8,128)}, u32[]{:S(2)}) %copy-start) | copy-done | bytes 3145752
  159.2 0.0 copy-start.1
  159.2 1.2 copy-done.1
  160.4 0.0 copy-start.2
  160.4 0.9 copy-done.2
  161.4 12.5 %solve.1 = (f32[1024,256]{1,0:T(8,128)}, f32[3,1024,256]{2,1,0:T(8,128)}) custom-call(f32[256,256]{1,0:T(8,128)S(1)} %bitcast.3, f32[1024,256]{1,0:T(8,128)S(1)} %bitcast.2, f32[3,1024,256]{2,1,0:T(8,128)S(1)} %copy-done), custom_call_target="tpu_custom_call" | custom-call | tf_op jit(solution)/shard_map/solve/pallas_call | solution.py:483
Async XLA Ops:
  157.3 1.9 %copy-start = (f32[3,1024,256]{2,1,0:T(8,128)S(1)}, f32[3,1024,256]{2,1,0:T(8,128)}, u32[]{:S(2)}) copy-start(f32[3,1024,256]{2,1,0:T(8,128)} %get-tuple-element.9.refs_2_) | copy-start | bytes 9437188
  159.2 1.2 copy-start.1
  160.4 0.9 copy-start.2

commit v4 on v3

--- a/solution.py
+++ b/solution.py
@@ -12,7 +12,7 @@
 F32 = jnp.float32
 BF16 = jnp.bfloat16
 NX, NZ, NY = 4, 8, 4
-SEMS = 256
+SEMS = 448
 
 
 class Clock:
@@ -20,9 +20,9 @@
         self.now, self.busy, self.flows = 0.0, {}, []
 
     def sent(self, axis, kib):
-        rate = 0.0068 if axis == "c" else 0.022
+        rate = 0.0087 if axis == "c" else 0.0225
         self.busy[axis] = max(self.now, self.busy.get(axis, 0.0)) + kib * rate
-        return self.busy[axis] + (1.0 if axis == "c" else 1.8)
+        return self.busy[axis] + (1.0 if axis == "c" else 1.9)
 
     def add(self, start, flow):
         self.flows.append([start, len(self.flows), flow])
@@ -30,7 +30,7 @@
     def run(self):
         while self.flows:
             item = min(self.flows)
-            self.now = max(self.now, item[0]) + 0.1
+            self.now = max(self.now, item[0]) + 0.08
             try:
                 item[0] = next(item[2])
             except StopIteration:
@@ -111,6 +111,9 @@
                     yield due[kind]
                 due[kind] = self.step(t, kind)
         yield max(due.values())
+        return self.final()
+
+    def final(self):
         last = self.half_ring
         out = []
         for h in (0, 1):
@@ -196,151 +199,200 @@
     return lax.dot_general(a, b, (((1,), (0,)), ((), ())), precision=HIGH, preferred_element_type=F32)
 
 
-def project(scale, widths, shared, inv, sketched, loadings, merged, gram,
-            feats, sharedT, terms, land_x, quarter, land_z, land_z2, quarter2, land_x2, proj, invx,
-            part, part_in, part_sum, land_h, half, back, land_b, loadT, stage,
+CHAINS = (
+    (0, 0, 0.0, "x", "z"), (0, 1, 0.01, "z", "z"), (1, 0, 0.02, "x", "z"),
+    (1, 1, 1.0, "z", "x"), (2, 0, 3.0, "x", "x"), (2, 1, 9.0, "z", "x"),
+)
+INV_START = 12.0
+
+
+def project(scale, widths, shared, inv, sketched, stage, merged, gram,
+            feats, sharedH, sharedT, terms, land_x, land_xz, land_z, land_zx, quarter, slab, proj, invx, hop,
+            part, part_in, part_sum, land_h, half, back, land_b, loadT,
             contrib, mine_in, mine_sum, land_m, outer, outer_in, outer_sum, from_y, over_x, over_z,
-            send_sems, recv_sems, feat_sems, out_sems, own_sem):
+            send_sems, recv_sems, feat_sems, own_sems):
     y, x, z, c = place()
     links = Links(send_sems, recv_sems)
     clock = links.clock
     rx, rz, ry = rings(links, x, z, y)
     partner = {"col": 1 - c}
 
+    bring_shared = pltpu.make_async_copy(shared, sharedH, own_sems.at[0])
+    bring_shared.start()
     barrier = pltpu.get_barrier_semaphore()
     peers = [partner] + [ring.device(d) for ring in (rx, rz, ry) for d in range(1, ring.size)]
     for peer in peers:
         pl.semaphore_signal(barrier, inc=1, device_id=peer, device_id_type=MESH)
 
+    def columns(q):
+        return pl.ds(pl.multiple_of(q * 256, 256), 256)
+
     quarters = [rx.at(d) for d in (2, 3, 1, 0)]
     loads = {}
-    for i, v in enumerate((2, 0, 1)):
+    for v in range(3):
         for n, q in enumerate(quarters):
-            loads[v, n] = pltpu.make_async_copy(
-                sketched.at[v, :, pl.ds(pl.multiple_of(q * 256, 256), 256)], feats.at[v, q],
-                feat_sems.at[4 * i + n])
+            loads[v, n] = pltpu.make_async_copy(sketched.at[v, :, columns(q)], feats.at[v, q], feat_sems.at[4 * v + n])
             loads[v, n].start()
-    own_inv = pltpu.make_async_copy(
-        inv.at[:, :, pl.ds(pl.multiple_of(x * 256, 256), 256)], invx.at[:, x], own_sem)
+    own_inv = pltpu.make_async_copy(inv.at[:, :, columns(x)], invx.at[:, x], own_sems.at[1])
     own_inv.start()
-    sharedT[...] = shared[...].T
+    bring_shared.wait()
+    sharedT[...] = sharedH[...].T
 
     first_col = c * 1024 + x * 256
-    lane = lax.broadcasted_iota(jnp.int32, (16, 256), 1)
+    lane = lax.broadcasted_iota(jnp.int32, (8, 256), 1)
     row = (lane // 64) * (64 * NZ) + z * 64 + lax.rem(lane, 64)
 
     def lanes_kept(v, value):
         return jnp.where(first_col + lane < widths[v], value, 0.0)
 
-    inv_slots = {}
-
-    def send_inv():
-        for d in (1, 3, 2):
-            inv_slots[d] = links.slot()
-            links.send(inv_slots[d], inv.at[:, :, pl.ds(pl.multiple_of(rx.at(d) * 256, 256), 256)],
-                       invx.at[:, x], rx.device(d))
-        clock.sent("x", 288)
-        yield clock.now
-
-    def need_inv():
-        if None not in inv_slots:
+    inv_slots = {(v, kind, i): links.slot() for v in range(3) for kind in ("near", "hop", "far") for i in (0, 1)}
+
+    def inv_flow():
+        for v in range(3):
+            for i, sign in enumerate((1, -1)):
+                links.send(inv_slots[v, "near", i], inv.at[v, :, columns(rx.at(sign))], invx.at[v, x], rx.device(sign))
+                links.send(inv_slots[v, "hop", i], inv.at[v, pl.ds(32 * i, 32), columns(rx.at(2))],
+                           hop.at[v, i], rx.device(sign))
+            due = clock.sent("x", 96)
+            yield clock.now
+        yield due
+        for v in range(3):
+            for i, sign in enumerate((1, -1)):
+                links.arrived(inv_slots[v, "hop", i], hop.at[v, i], rx.device(sign))
+                links.send(inv_slots[v, "far", i], hop.at[v, i], invx.at[v, rx.at(-sign), pl.ds(32 * i, 32)],
+                           rx.device(sign))
+            due = clock.sent("x", 32)
+            yield clock.now
+
+    sending_inv = inv_flow()
+    inv_here = set()
+
+    def need_inv(v):
+        for _ in sending_inv:
+            pass
+        if not inv_here:
             own_inv.wait()
-            for d in (1, 3, 2):
-                links.arrived(inv_slots[d], invx.at[:, rx.at(-d)], rx.device(d))
-            inv_slots[None] = None
+        if v not in inv_here:
+            inv_here.add(v)
+            for i, sign in enumerate((1, -1)):
+                links.arrived(inv_slots[v, "near", i], invx.at[v, rx.at(-sign)], rx.device(sign))
+                links.arrived(inv_slots[v, "far", i], invx.at[v, rx.at(2), pl.ds(32 * i, 32)], rx.device(sign))
 
     def swap(src, dst, landed):
         slot = links.slot()
         links.send(slot, src, dst, partner)
-        yield clock.sent("c", 128)
+        yield clock.sent("c", 64)
         links.arrived(slot, landed, partner)
 
-    outs = []
-
-    def use(v, q):
-        block = loadT[v, q].reshape(256, 256).T
-        stage[v, q] = block
-        out = pltpu.make_async_copy(
-            stage.at[v, q], loadings.at[v, pl.ds(pl.multiple_of(q * 256, 256), 256)], out_sems.at[len(outs)])
-        out.start()
-        product = jnp.dot(feats[v, q], block.astype(BF16), preferred_element_type=F32).reshape(2, NY, 128, 256)
-        contrib[...] = contrib[...] + product if outs else product
-        outs.append(out)
-
-    def reached_x(v, t):
-        for d in sorted({t % NX, -t % NX}):
-            use(v, rx.at(d))
-
-    def view_flow(v):
+    used = []
+
+    def use(v, k, q):
+        block = loadT[v, k, q].reshape(128, 256).T
+        stage[v, columns(q), 128 * k:128 * k + 128] = block
+        product = jnp.dot(feats[v, q], block.astype(BF16), preferred_element_type=F32).reshape(2, NY, 128, 128)
+        here = slice(128 * k, 128 * k + 128)
+        contrib[:, :, :, here] = contrib[:, :, :, here] + product if k in used else product
+        used.append(k)
+
+    made = set()
+
+    def make_terms(v):
+        if v in made:
+            return
+        made.add(v)
         for n, q in enumerate(quarters):
             loads[v, n].wait()
-            terms[v, q] = jnp.dot(sharedT[...], feats[v, q], preferred_element_type=F32).reshape(NZ, 32, 256)
-        if v == 2:
+            terms[v, :, q] = jnp.dot(sharedT[...], feats[v, q], preferred_element_type=F32).reshape(2, NZ, 16, 256)
+        if len(made) == 1:
             pl.semaphore_wait(barrier, len(peers))
+
+    def chain(v, k, first, last):
+        make_terms(v)
+        if first == "x":
             halves = yield from ReduceScatter(
-                rz, lambda o, h: terms.at[2, :, o, pl.ds(16 * h, 16)], land_z2, 64).flow()
+                rx, lambda o, h: terms.at[v, k, o, pl.ds(4 * h, 4)], land_x.at[v, k], 64).flow()
             for h in (0, 1):
-                quarter2[:, pl.ds(16 * h, 16)] = halves[h]
-            halves = yield from ReduceScatter(rx, lambda o, h: quarter2.at[o, pl.ds(16 * h, 16)], land_x2, 16).flow()
+                quarter[v, k, pl.ds(4 * h, 4)] = halves[h]
+            halves = yield from ReduceScatter(
+                rz, lambda o, h: quarter.at[v, k, o, pl.ds(8 * h, 8)], land_xz.at[v, k], 8).flow()
         else:
             halves = yield from ReduceScatter(
-                rx, lambda o, h: terms.at[v, o, pl.ds(4 * h, 4)], land_x.at[v], 128).flow()
+                rz, lambda o, h: terms.at[v, k, :, o, pl.ds(8 * h, 8)], land_z.at[v, k], 32).flow()
             for h in (0, 1):
-                quarter[v, pl.ds(4 * h, 4)] = halves[h]
+                slab[v, k, :, pl.ds(8 * h, 8)] = halves[h]
             halves = yield from ReduceScatter(
-                rz, lambda o, h: quarter.at[v, o, pl.ds(16 * h, 16)], land_z.at[v], 16).flow()
+                rx, lambda o, h: slab.at[v, k, o, pl.ds(8 * h, 8)], land_zx.at[v, k], 8).flow()
         for h in (0, 1):
-            proj[v, z, pl.ds(16 * h, 16)] = lanes_kept(v, halves[h] * scale)
-        yield from AllGather(rz, lambda o: proj.at[v, o], lambda o, h: proj.at[v, o, pl.ds(16 * h, 16)], 32).flow()
-
-        need_inv()
-        part[v] = nt(proj[v].reshape(256, 256), invx[v].reshape(256, 256)).reshape(2, NX, 32, 256)
-        yield from swap(part.at[v, 1 - c], part_in.at[v], part_in.at[v])
-        part_sum[v] = part[v, c] + part_in[v]
+            proj[v, k, z, pl.ds(8 * h, 8)] = lanes_kept(v, halves[h] * scale)
+        yield from AllGather(
+            rz, lambda o: proj.at[v, k, o], lambda o, h: proj.at[v, k, o, pl.ds(8 * h, 8)], 16).flow()
+
+        need_inv(v)
+        part[v, k] = nt(proj[v, k].reshape(128, 256), invx[v].reshape(256, 256)).reshape(2, NX, 16, 256)
+        yield from swap(part.at[v, k, 1 - c], part_in.at[v, k], part_in.at[v, k])
+        part_sum[v, k] = part[v, k, c] + part_in[v, k]
         halves = yield from ReduceScatter(
-            rx, lambda o, h: part_sum.at[v, o, pl.ds(16 * h, 16)], land_h.at[v], 16).flow()
+            rx, lambda o, h: part_sum.at[v, k, o, pl.ds(8 * h, 8)], land_h.at[v, k], 8).flow()
         for h in (0, 1):
-            half[v, c, x, pl.ds(16 * h, 16)] = jnp.where(row < widths[v], halves[h], 0.0)
-        yield from AllGather(rx, lambda o: half.at[v, c, o], lambda o, h: half.at[v, c, o, pl.ds(16 * h, 16)], 32).flow()
-        yield from swap(half.at[v, c], half.at[v, c], half.at[v, 1 - c])
-
-        back[v] = nn(half[v].reshape(256, 256), invx[v].reshape(256, 256)).reshape(NZ, 32, 256)
+            half[v, k, c, x, pl.ds(8 * h, 8)] = jnp.where(row < widths[v], halves[h], 0.0)
+        yield from AllGather(
+            rx, lambda o: half.at[v, k, c, o], lambda o, h: half.at[v, k, c, o, pl.ds(8 * h, 8)], 16).flow()
+        yield from swap(half.at[v, k, c], half.at[v, k, c], half.at[v, k, 1 - c])
+
+        back[v, k] = nn(half[v, k].reshape(128, 256), invx[v].reshape(256, 256)).reshape(NZ, 16, 256)
         halves = yield from ReduceScatter(
-            rz, lambda o, h: back.at[v, o, pl.ds(16 * h, 16)], land_b.at[v], 16).flow()
+            rz, lambda o, h: back.at[v, k, o, pl.ds(8 * h, 8)], land_b.at[v, k], 8).flow()
         for h in (0, 1):
-            loadT[v, x, z, pl.ds(16 * h, 16)] = lanes_kept(v, halves[h])
-        if v == 2:
-            yield from AllGather(rx, lambda o: loadT.at[2, o, z], lambda o, h: loadT.at[2, o, z, pl.ds(16 * h, 16)], 32).flow()
-            yield from AllGather(rz, lambda o: loadT.at[2, :, o], lambda o, h: loadT.at[2, :, o, pl.ds(16 * h, 16)], 128).flow()
+            loadT[v, k, x, z, pl.ds(8 * h, 8)] = lanes_kept(v, halves[h])
+        if last == "x":
+            yield from AllGather(
+                rx, lambda o: loadT.at[v, k, o, z], lambda o, h: loadT.at[v, k, o, z, pl.ds(8 * h, 8)], 16).flow()
+            yield from AllGather(
+                rz, lambda o: loadT.at[v, k, :, o], lambda o, h: loadT.at[v, k, :, o, pl.ds(8 * h, 8)], 64).flow()
             for q in range(NX):
-                use(2, q)
+                use(v, k, q)
         else:
-            yield from AllGather(rz, lambda o: loadT.at[v, x, o], lambda o, h: loadT.at[v, x, o, pl.ds(16 * h, 16)], 32).flow()
             yield from AllGather(
-                rx, lambda o: loadT.at[v, o], lambda o, h: loadT.at[v, o, pl.ds(4 * h, 4)], 256,
-            ).flow(lambda t: reached_x(v, t))
-
-    clock.add(0.0, view_flow(2))
-    clock.add(0.5, view_flow(0))
-    clock.add(5.5, view_flow(1))
-    clock.add(16.0, send_inv())
+                rz, lambda o: loadT.at[v, k, x, o], lambda o, h: loadT.at[v, k, x, o, pl.ds(8 * h, 8)], 16).flow()
+
+            def reached(t):
+                for d in sorted({t % NX, -t % NX}):
+                    use(v, k, rx.at(d))
+
+            yield from AllGather(
+                rx, lambda o: loadT.at[v, k, o], lambda o, h: loadT.at[v, k, o, pl.ds(4 * h, 4)], 128).flow(reached)
+
+    for v, k, start, first, last in CHAINS:
+        clock.add(start, chain(v, k, first, last))
+    clock.add(INV_START, sending_inv)
     clock.run()
 
-    def now(flow):
-        try:
-            while True:
-                next(flow)
-        except StopIteration as stop:
-            return stop.value
-
-    now(swap(contrib.at[1 - c], mine_in, mine_in))
-    mine_sum[...] = contrib[c] + mine_in[...]
-    halves = now(ReduceScatter(ry, lambda o, h: mine_sum.at[o, pl.ds(64 * h, 64)], land_m, 64).flow())
+    slots = {d: links.slot() for d in (2, 1, 3, 0)}
+    for d, slot in slots.items():
+        links.send(slot, contrib.at[1 - c, ry.at(d)], mine_in.at[ry.at(d)], partner)
+
+    def summed(d):
+        o = ry.at(d)
+        links.arrived(slots[d], mine_in.at[o], partner)
+        mine_sum[o] = contrib[c, o] + mine_in[o]
+
+    ms = ReduceScatter(ry, lambda o, h: mine_sum.at[o, pl.ds(64 * h, 64)], land_m, 64)
+    summed(2)
+    ms.step(1, 0)
+    summed(1)
+    summed(3)
+    ms.step(1, 1)
+    summed(0)
+    ms.step(2, 0)
+    halves = ms.final()
     for h in (0, 1):
         merged[c, y, pl.ds(64 * h, 64)] = halves[h]
     rows = merged[c, y]
+
     outer[...] = tn(rows, rows).reshape(2, NY, 32, 256)
-    now(swap(outer.at[1 - c], outer_in, outer_in))
+    slot = links.slot()
+    links.send(slot, outer.at[1 - c], outer_in, partner)
+    links.arrived(slot, outer_in, partner)
     outer_sum[...] = outer[c] + outer_in[...]
     gs = Direct(ry, lambda o: outer_sum.at[o], lambda o: from_y.at[o])
     mg = AllGather(ry, lambda o: merged.at[c, o], lambda o, h: merged.at[c, o, pl.ds(64 * h, 64)], 128)
@@ -361,11 +413,11 @@
         acc = acc + over_z[i]
     gram[c, y] = acc
     Direct(ry, lambda o: gram.at[c, y], lambda o: gram.at[c, o]).final()
-    now(swap(gram.at[c], gram.at[c], gram.at[1 - c]))
+    last = links.slot()
+    links.send(last, gram.at[c], gram.at[c], partner)
+    links.arrived(last, gram.at[1 - c], partner)
     links.arrived(slot, merged.at[1 - c], partner)
     links.drain()
-    for out in outs:
-        out.wait()
 
 
 PANEL = 32
@@ -405,7 +457,7 @@
     return lax.dot_general(a, b, (((0,), (0,)), ((), ())), precision=HIGH, preferred_element_type=F32)
 
 
-def factor_inverse(work, inverse, between):
+def factor_inverse(work, inverse):
     n = work.shape[0]
     for p in range(n // PANEL):
         r0 = p * PANEL
@@ -418,7 +470,6 @@
         wide = jnp.where(here, jnp.where(col == row + r0, 1.0, 0.0), work[r0:r0 + PANEL, :])
         u = nn(block, wide)
         inverse[r0:r0 + PANEL, :] = jnp.where(col < r0 + PANEL, u, 0.0)
-        between(p)
         r1 = r0 + PANEL
         if r1 < n:
             base = r1 // 128 * 128
@@ -428,25 +479,18 @@
             work[r1:, :] = jnp.where(here, 0.0, work[r1:, :]) - upd
 
 
-def solve(root, gram, merged, loaded, updated, loadings, work, inverse, passing, in_sem, out_sem):
-    bring = pltpu.make_async_copy(loaded, passing, in_sem)
-    put = pltpu.make_async_copy(passing, loadings, out_sem)
-    bring.start()
+def solve(root, gram, merged, loaded, updated, loadings, work, inverse, sem):
+    put = pltpu.make_async_copy(loaded, loadings, sem)
+    put.start()
     work[...] = gram[...]
-
-    def between(panel):
-        if panel == 2:
-            bring.wait()
-            put.start()
-
-    factor_inverse(work, inverse, between)
+    factor_inverse(work, inverse)
     updated[...] = nt(merged[...], inverse[...]) * root
     put.wait()
 
 
 def shards(sketched, widths, inv_factor, shared):
     total_rows = shared.shape[0] * lax.axis_size("sent")
-    vmem, smem, anywhere = (pl.BlockSpec(memory_space=m) for m in (pltpu.VMEM, pltpu.SMEM, pl.ANY))
+    vmem, smem, hbm = (pl.BlockSpec(memory_space=m) for m in (pltpu.VMEM, pltpu.SMEM, pltpu.HBM))
 
     def buf(*shape):
         return pltpu.VMEM(shape, F32)
@@ -456,24 +500,24 @@
     def kernel_a(*refs):
         project(1.0 / math.sqrt(total_rows), *refs)
 
-    loadings, merged, gram = pl.pallas_call(
+    stage, merged, gram = pl.pallas_call(
         kernel_a,
         name="project",
         out_shape=(jax.ShapeDtypeStruct((3, 1024, 256), F32), jax.ShapeDtypeStruct((2, NY, 128, 256), F32),
                    jax.ShapeDtypeStruct((2, NY, 32, 256), F32)),
-        in_specs=[smem, vmem, vmem, anywhere],
-        out_specs=(anywhere, vmem, vmem),
+        in_specs=[smem, hbm, hbm, hbm],
+        out_specs=(vmem, vmem, vmem),
         scratch_shapes=[
-            pltpu.VMEM((3, 4, 1024, 256), BF16), pltpu.VMEM((256, 1024), BF16),
-            buf(3, 4, 8, 32, 256), buf(2, 2, 2, 2, 4, 32, 256), buf(2, 8, 32, 256), buf(2, 2, 2, 4, 16, 256),
-            buf(2, 2, 4, 4, 16, 256), buf(4, 32, 256), buf(2, 2, 2, 16, 256), buf(3, 8, 32, 256),
-            buf(3, 4, 64, 256), buf(3, 2, 4, 32, 256), buf(3, 4, 32, 256), buf(3, 4, 32, 256),
-            buf(3, 2, 2, 2, 16, 256), buf(3, 2, 4, 32, 256), buf(3, 8, 32, 256), buf(3, 2, 2, 4, 16, 256),
-            buf(3, 4, 8, 32, 256), buf(3, 4, 256, 256),
+            pltpu.VMEM((3, 4, 1024, 256), BF16), pltpu.VMEM((1024, 256), BF16), pltpu.VMEM((256, 1024), BF16),
+            buf(3, 2, 4, 8, 16, 256), buf(3, 2, 2, 2, 2, 4, 16, 256), buf(3, 2, 2, 2, 4, 8, 256),
+            buf(3, 2, 2, 2, 4, 4, 8, 256), buf(3, 2, 2, 2, 2, 8, 256), buf(3, 2, 8, 16, 256), buf(3, 2, 4, 16, 256),
+            buf(3, 2, 8, 16, 256), buf(3, 4, 64, 256), buf(3, 2, 32, 256),
+            buf(3, 2, 2, 4, 16, 256), buf(3, 2, 4, 16, 256), buf(3, 2, 4, 16, 256), buf(3, 2, 2, 2, 2, 8, 256),
+            buf(3, 2, 2, 4, 16, 256), buf(3, 2, 8, 16, 256), buf(3, 2, 2, 2, 4, 8, 256), buf(3, 2, 4, 8, 16, 256),
             buf(2, 4, 128, 256), buf(4, 128, 256), buf(4, 128, 256), buf(2, 2, 2, 64, 256), buf(2, 4, 32, 256),
             buf(4, 32, 256), buf(4, 32, 256), buf(4, 32, 256), buf(4, 32, 256), buf(8, 32, 256), *sems,
-            pltpu.SemaphoreType.DMA((12,)), pltpu.SemaphoreType.DMA((12,)), pltpu.SemaphoreType.DMA],
-        compiler_params=pltpu.CompilerParams(collective_id=0, has_side_effects=True, vmem_limit_bytes=56 * 2**20),
+            pltpu.SemaphoreType.DMA((12,)), pltpu.SemaphoreType.DMA((2,))],
+        compiler_params=pltpu.CompilerParams(collective_id=0, has_side_effects=True, vmem_limit_bytes=44 * 2**20),
     )(widths, shared, inv_factor, sketched)
     merged, gram = merged.reshape(1024, 256), gram.reshape(256, 256)
 
@@ -484,12 +528,11 @@
         kernel_c,
         name="solve",
         out_shape=(jax.ShapeDtypeStruct((1024, 256), F32), jax.ShapeDtypeStruct((3, 1024, 256), F32)),
-        in_specs=[vmem, vmem, anywhere],
-        out_specs=(vmem, anywhere),
-        scratch_shapes=[buf(256, 256), buf(256, 256), buf(3, 1024, 256),
-                        pltpu.SemaphoreType.DMA, pltpu.SemaphoreType.DMA],
-        compiler_params=pltpu.CompilerParams(vmem_limit_bytes=32 * 2**20),
-    )(gram, merged, loadings)
+        in_specs=[vmem, vmem, vmem],
+        out_specs=(vmem, hbm),
+        scratch_shapes=[buf(256, 256), buf(256, 256), pltpu.SemaphoreType.DMA],
+        compiler_params=pltpu.CompilerParams(vmem_limit_bytes=16 * 2**20),
+    )(gram, merged, stage)
     return (loadings, updated)
 
 

time: 174 us -> 164 us (0.943)
  Pallas kernels: 169 us -> 160 us
    pallas_call x1, Pallas kernels: 157 us -> 149 us  [shards(): pl.pallas_call(kernel_a, name='project', out_shape=(jax.ShapeDtypeStruct(...]
where the time goes in v4:
time: 164 us; the launch traced here: 163 us
  Pallas kernels  160 us (98%)
  local copies, waits for them, and re-layouts  2.82 us (2%)
    pallas_call x1, Pallas kernels, shards(): pl.pallas_call(kernel_a, name='project', out_shape=(jax.ShapeDtypeStruct(...  149 us
    pallas_call x1, Pallas kernels, shards(): pl.pallas_call(kernel_c, name='solve', out_shape=(jax.ShapeDtypeStruct((1...  11.2 us

profile of v4, /device:TPU:1, one launch (start us, length us, event | category | flops | bytes accessed | tf_op | source)
XLA Modules:
  0.0 163.4 jit_solution(5669375620944532222)
XLA Ops:
  0.6 0.0 copy-start
  0.6 1.1 copy-done
  1.8 0.0 copy-start.1
  1.8 1.0 copy-done.1
  2.8 0.0 copy-start.2
  2.8 0.7 copy-done.2
  3.5 148.6 %project.1 = (f32[3,1024,256]{2,1,0:T(8,128)S(1)}, f32[2,4,128,256]{3,2,1,0:T(8,128)S(1)}, f32[2,4,32,256]{3,2,1,0:T(8,128)S(1)}) custom-call(s32[3]{0:T(128)S(1)} %copy-done.2, bf16[1024,256]{1,0:T(8,128)(2,1)S(1)} %copy-done.1, f32[3,64,1024]{2,1,0:T(8,128)S(1)} %copy-done, bf16[3,1024,1024]{2,1,0:T(8,128)(2,1)} %refs_3_.1), custom_call_target="tpu_custom_call" | custom-call | tf_op jit(solution)/shard_map/project/pallas_call | solution.py:503
  152.1 11.2 %solve.1 = (f32[1024,256]{1,0:T(8,128)}, f32[3,1024,256]{2,1,0:T(8,128)}) custom-call(f32[256,256]{1,0:T(8,128)S(1)} %bitcast.3, f32[1024,256]{1,0:T(8,128)S(1)} %bitcast.2, f32[3,1024,256]{2,1,0:T(8,128)S(1)} %get-tuple-element.9.refs_2_), custom_call_target="tpu_custom_call" | custom-call | tf_op jit(solution)/shard_map/solve/pallas_call | solution.py:527
Async XLA Ops:
  0.6 1.1 copy-start
  1.8 1.0 copy-start.1
  2.8 0.7 copy-start.2

commit v5 on v4

v5 whole, which is shorter than its diff:
```python
import math

import jax
import jax.numpy as jnp
from jax import lax
from jax.experimental import pallas as pl
from jax.experimental.pallas import tpu as pltpu
from jax.sharding import PartitionSpec as P

MESH = pl.DeviceIdType.MESH
HIGH = lax.Precision.HIGHEST
F32 = jnp.float32
BF16 = jnp.bfloat16
NX, NZ, NY = 4, 8, 4
SEND_SEMS, RECV_SEMS = 40, 224


class Clock:
    def __init__(self):
        self.now, self.busy, self.flows = 0.0, {}, []

    def sent(self, axis, kib, latency=2.4):
        self.busy[axis] = max(self.now, self.busy.get(axis, 0.0)) + kib * 0.0225
        return self.busy[axis] + latency

    def add(self, start, flow):
        self.flows.append([start, len(self.flows), flow])

    def run(self):
        while self.flows:
            item = min(self.flows)
            self.now = max(self.now, item[0]) + 0.1
            try:
                item[0] = next(item[2])
            except StopIteration:
                self.flows.remove(item)


def kib(ref):
    return math.prod(ref.shape) * 4 // 1024


class Links:
    def __init__(self, send_sems, recv_sems, ruler):
        self.send_sems, self.recv_sems, self.ruler = send_sems, recv_sems, ruler
        self.used, self.groups, self.clock = 0, [], Clock()

    def slot(self):
        self.used += 1
        assert self.used <= RECV_SEMS
        return self.used - 1

    def send(self, slot, src, dst, device):
        size = kib(src)
        if not self.groups or self.groups[-1] + size > 1024:
            self.groups.append(0)
            assert len(self.groups) <= SEND_SEMS
        self.groups[-1] += size
        pltpu.make_async_remote_copy(
            src_ref=src, dst_ref=dst, send_sem=self.send_sems.at[len(self.groups) - 1],
            recv_sem=self.recv_sems.at[slot], device_id=device, device_id_type=MESH).start()

    def wait(self, sem, size):
        rows = self.ruler.at[0, pl.ds(0, size)]
        pltpu.make_async_copy(rows, rows, sem).wait()

    def arrived(self, slot, size):
        self.wait(self.recv_sems.at[slot], size)

    def drain(self):
        for group, size in enumerate(self.groups):
            self.wait(self.send_sems.at[group], size)


class Ring:
    def __init__(self, links, axis, size, pos, device):
        self.links, self.axis, self.size, self.pos, self.device = links, axis, size, pos, device

    def at(self, delta):
        return lax.rem(self.pos + (delta % self.size), self.size)


class ReduceScatter:
    def __init__(self, ring, own, landing):
        self.ring, self.own, self.landing = ring, own, landing
        self.kib = kib(landing.at[0, 0, 0])
        self.half_ring = ring.size // 2
        self.slots = {(kind, t): ring.links.slot()
                      for t in range(1, self.half_ring + 1) for kind in (0, 1)
                      if not (kind == 1 and t == self.half_ring)}

    def wait(self, kind, t):
        self.ring.links.arrived(self.slots[kind, t], 2 * self.kib)

    def step(self, t, kind):
        if t > 1:
            self.wait(kind, t - 1)
        for d, sign in ((0, -1), (1, 1)):
            dist = self.half_ring + 1 - t - kind
            src = self.own(self.ring.at(sign * dist), d if kind == 0 else 1 - d)
            if t > 1:
                buf = self.landing.at[d, kind, t - 2]
                buf[...] = buf[...] + src[...]
                src = buf
            self.ring.links.send(self.slots[kind, t], src, self.landing.at[d, kind, t - 1], self.ring.device(sign))
        return self.ring.links.clock.sent(self.ring.axis, self.kib)

    def flow(self):
        due = {}
        for t in range(1, self.half_ring + 1):
            for kind in (0, 1):
                if (kind, t) not in self.slots:
                    continue
                if t > 1:
                    yield due[kind]
                due[kind] = self.step(t, kind)
        yield max(due.values())
        return self.final()

    def final(self):
        last = self.half_ring
        self.wait(0, last)
        self.wait(1, last - 1)
        return [self.own(self.ring.pos, h)[...] + self.landing[h, 0, last - 1] + self.landing[1 - h, 1, last - 2]
                for h in (0, 1)]


class AllGather:
    def __init__(self, ring, full, half):
        self.ring, self.full, self.half = ring, full, half
        self.kib = kib(full(ring.pos))
        self.half_ring = ring.size // 2
        self.slots = {t: ring.links.slot() for t in range(1, self.half_ring + 1)}

    def wait(self, t):
        self.ring.links.arrived(self.slots[t], 2 * self.kib if t < self.half_ring else self.kib)

    def step(self, t):
        if t > 1:
            self.wait(t - 1)
        for d, sign in ((0, -1), (1, 1)):
            owner = self.ring.at(-sign * (t - 1))
            src = self.half(owner, d) if t == self.half_ring else self.full(owner)
            self.ring.links.send(self.slots[t], src, src, self.ring.device(sign))
        return self.ring.links.clock.sent(self.ring.axis, self.kib if t < self.half_ring else self.kib / 2)

    def final(self):
        self.wait(self.half_ring)

    def flow(self, reached=None):
        for t in range(1, self.half_ring + 1):
            due = self.step(t)
            if reached is not None:
                reached(t - 1)
            yield due
        self.final()
        if reached is not None:
            reached(self.half_ring)


class Direct:
    def __init__(self, ring, source, target):
        links = self.links = ring.links
        order = sorted(range(1, ring.size), key=lambda d: -min(d, ring.size - d))
        self.slot, self.kib = links.slot(), kib(source(ring.pos))
        self.total = self.kib * len(order)
        for d in order:
            links.send(self.slot, source(ring.at(d)), target(ring.pos, d), ring.device(d))
        wide = ring.size > 4
        self.due = links.clock.sent(ring.axis, self.kib * (9 if wide else 3), 1.9 if wide else 2.6)

    def final(self):
        self.links.arrived(self.slot, self.total)


def summed_block(ring, own, landing, relay, direct):
    if not direct:
        halves = yield from ReduceScatter(ring, own, relay).flow()
        return halves
    whole = own(ring.pos, None)
    moved = Direct(ring, lambda o: own(o, None), lambda o, d: landing.at[d])
    yield moved.due
    moved.final()
    total = whole[...]
    for d in range(1, ring.size):
        total = total + landing[d]
    return [total[:8], total[8:]]


def gathered(ring, full, half, direct):
    if not direct:
        yield from AllGather(ring, full, half).flow()
    else:
        moved = Direct(ring, lambda o: full(ring.pos), lambda o, d: full(o))
        yield moved.due
        moved.final()


def rows8(h):
    return slice(None) if h is None else pl.ds(8 * h, 8)


def place():
    y, s, c = lax.axis_index("view"), lax.axis_index("sent"), lax.axis_index("col")
    return y, s // NZ, lax.rem(s, NZ), c


def rings(links, x, z, y):
    def x_dev(delta):
        return {"sent": lax.rem(x + (delta % NX), NX) * NZ + z}

    def z_dev(delta):
        return {"sent": x * NZ + lax.rem(z + (delta % NZ), NZ)}

    def y_dev(delta):
        return {"view": lax.rem(y + (delta % NY), NY)}

    return (Ring(links, "x", NX, x, x_dev), Ring(links, "z", NZ, z, z_dev), Ring(links, "y", NY, y, y_dev))


def nt(a, b):
    return lax.dot_general(a, b, (((1,), (1,)), ((), ())), precision=HIGH, preferred_element_type=F32)


def nn(a, b):
    return lax.dot_general(a, b, (((1,), (0,)), ((), ())), precision=HIGH, preferred_element_type=F32)


CHAINS = (
    (0, 0, 0.02, "z", "z", (True, False, True, True, True, False)),
    (0, 1, 1.01, "x", "z", (True, False, False, False, True, False)),
    (1, 0, 2.03, "x", "x", (False, True, True, True, False, True)),
    (1, 1, 2.05, "z", "z", (False, True, False, True, True, False)),
    (2, 0, 10.04, "z", "x", (True, True, True, True, True, True)),
    (2, 1, 11.0, "x", "x", (False, True, True, False, True, True)),
)
INV_START = 15.0


def project(scale, widths, shared, inv, sketched, loadings, merged_out, gram_out,
            feats, sharedH, sharedT, terms, land_x, land_xz, land_z, land_zx, quarter, slab, proj, invx, hop,
            part, part_in, part_sum, land_h, half, back, land_b, loadT, stage, merged, gram, land_8, land_4,
            contrib, mine_in, mine_sum, land_m, outer, outer_in, outer_sum, from_y, over_x, over_z,
            send_sems, recv_sems, feat_sems, own_sems, out_sems):
    y, x, z, c = place()
    links = Links(send_sems, recv_sems, stage)
    clock = links.clock
    rx, rz, ry = rings(links, x, z, y)
    partner = {"col": 1 - c}

    bring_shared = pltpu.make_async_copy(shared, sharedH, own_sems.at[0])
    bring_shared.start()
    barrier = pltpu.get_barrier_semaphore()
    peers = [partner] + [ring.device(d) for ring in (rx, rz, ry) for d in range(1, ring.size)]
    for peer in peers:
        pl.semaphore_signal(barrier, inc=1, device_id=peer, device_id_type=MESH)

    def columns(q):
        return pl.ds(pl.multiple_of(q * 256, 256), 256)

    quarters = [rx.at(d) for d in (2, 3, 1, 0)]
    loads = {}
    for v in range(3):
        for n, q in enumerate(quarters):
            loads[v, n] = pltpu.make_async_copy(sketched.at[v, :, columns(q)], feats.at[v, q], feat_sems.at[4 * v + n])
            loads[v, n].start()
    own_inv = pltpu.make_async_copy(inv.at[:, :, columns(x)], invx.at[:, x], own_sems.at[1])
    own_inv.start()
    bring_shared.wait()
    sharedT[...] = sharedH[...].T

    first_col = c * 1024 + x * 256
    lane = lax.broadcasted_iota(jnp.int32, (8, 256), 1)
    row = (lane // 64) * (64 * NZ) + z * 64 + lax.rem(lane, 64)

    def lanes_kept(v, value):
        return jnp.where(first_col + lane < widths[v], value, 0.0)

    inv_slots = {(v, kind): links.slot() for v in range(3) for kind in ("near", "hop", "far")}

    def inv_flow():
        for v in range(3):
            for i, sign in enumerate((1, -1)):
                links.send(inv_slots[v, "near"], inv.at[v, :, columns(rx.at(sign))], invx.at[v, x], rx.device(sign))
                links.send(inv_slots[v, "hop"], inv.at[v, pl.ds(32 * i, 32), columns(rx.at(2))],
                           hop.at[v, i], rx.device(sign))
            due = clock.sent("x", 96)
            yield clock.now
        yield due
        for v in range(3):
            links.arrived(inv_slots[v, "hop"], 64)
            for i, sign in enumerate((1, -1)):
                links.send(inv_slots[v, "far"], hop.at[v, i], invx.at[v, rx.at(-sign), pl.ds(32 * i, 32)],
                           rx.device(sign))
            due = clock.sent("x", 32)
            yield clock.now

    sending_inv = inv_flow()
    inv_here = set()

    def need_inv(v):
        for _ in sending_inv:
            pass
        if not inv_here:
            own_inv.wait()
        if v not in inv_here:
            inv_here.add(v)
            links.arrived(inv_slots[v, "near"], 128)
            links.arrived(inv_slots[v, "far"], 64)

    def swap(src, dst):
        slot = links.slot()
        links.send(slot, src, dst, partner)
        yield clock.now + 1.55
        links.arrived(slot, kib(src))

    used = []

    def use(v, k, q):
        block = loadT[v, k, q].reshape(128, 256).T
        stage[v, columns(q), 128 * k:128 * k + 128] = block
        product = jnp.dot(feats[v, q], block.astype(BF16), preferred_element_type=F32).reshape(2, NY, 128, 128)
        here = slice(128 * k, 128 * k + 128)
        contrib[:, :, :, here] = contrib[:, :, :, here] + product if k in used else product
        used.append(k)

    made = set()

    def make_terms(v):
        if v in made:
            return
        made.add(v)
        for n, q in enumerate(quarters):
            loads[v, n].wait()
            terms[v, :, q] = jnp.dot(sharedT[...], feats[v, q], preferred_element_type=F32).reshape(2, NZ, 16, 256)
        if len(made) == 1:
            pl.semaphore_wait(barrier, len(peers))

    def chain(v, k, first, last, direct):
        make_terms(v)
        if first == "x":
            halves = yield from ReduceScatter(
                rx, lambda o, h: terms.at[v, k, o, pl.ds(4 * h, 4)], land_x.at[v, k]).flow()
            for h in (0, 1):
                quarter[v, k, pl.ds(4 * h, 4)] = halves[h]
            halves = yield from summed_block(
                rz, lambda o, h: quarter.at[v, k, o, rows8(h)], land_8.at[v, k, 0], land_xz.at[v, k], direct[0])
        else:
            halves = yield from ReduceScatter(
                rz, lambda o, h: terms.at[v, k, :, o, pl.ds(8 * h, 8)], land_z.at[v, k]).flow()
            for h in (0, 1):
                slab[v, k, :, pl.ds(8 * h, 8)] = halves[h]
            halves = yield from summed_block(
                rx, lambda o, h: slab.at[v, k, o, rows8(h)], land_4.at[v, k, 0], land_zx.at[v, k], direct[0])
        for h in (0, 1):
            proj[v, k, z, pl.ds(8 * h, 8)] = lanes_kept(v, halves[h] * scale)
        yield from gathered(rz, lambda o: proj.at[v, k, o], lambda o, h: proj.at[v, k, o, rows8(h)], direct[1])

        need_inv(v)
        part[v, k] = nt(proj[v, k].reshape(128, 256), invx[v].reshape(256, 256)).reshape(2, NX, 16, 256)
        yield from swap(part.at[v, k, 1 - c], part_in.at[v, k])
        part_sum[v, k] = part[v, k, c] + part_in[v, k]
        halves = yield from summed_block(
            rx, lambda o, h: part_sum.at[v, k, o, rows8(h)], land_4.at[v, k, 1], land_h.at[v, k], direct[2])
        for h in (0, 1):
            half[v, k, c, x, pl.ds(8 * h, 8)] = jnp.where(row < widths[v], halves[h], 0.0)
        yield from gathered(rx, lambda o: half.at[v, k, c, o], lambda o, h: half.at[v, k, c, o, rows8(h)], direct[3])
        yield from swap(half.at[v, k, c], half.at[v, k, c])

        back[v, k] = nn(half[v, k].reshape(128, 256), invx[v].reshape(256, 256)).reshape(NZ, 16, 256)
        halves = yield from summed_block(
            rz, lambda o, h: back.at[v, k, o, rows8(h)], land_8.at[v, k, 1], land_b.at[v, k], direct[4])
        for h in (0, 1):
            loadT[v, k, x, z, pl.ds(8 * h, 8)] = lanes_kept(v, halves[h])
        if last == "x":
            yield from gathered(
                rx, lambda o: loadT.at[v, k, o, z], lambda o, h: loadT.at[v, k, o, z, rows8(h)], direct[5])
            yield from AllGather(
                rz, lambda o: loadT.at[v, k, :, o], lambda o, h: loadT.at[v, k, :, o, pl.ds(8 * h, 8)]).flow()
            for q in range(NX):
                use(v, k, q)
        else:
            yield from gathered(
                rz, lambda o: loadT.at[v, k, x, o], lambda o, h: loadT.at[v, k, x, o, rows8(h)], direct[5])

            def reached(t):
                for d in sorted({t % NX, -t % NX}):
                    use(v, k, rx.at(d))

            yield from AllGather(
                rx, lambda o: loadT.at[v, k, o], lambda o, h: loadT.at[v, k, o, pl.ds(4 * h, 4)]).flow(reached)

    for v, k, start, first, last, direct in CHAINS:
        clock.add(start, chain(v, k, first, last, direct))
    clock.add(INV_START, sending_inv)
    clock.run()
    put_loadings = pltpu.make_async_copy(stage, loadings, out_sems.at[0])
    put_loadings.start()

    slots = {d: links.slot() for d in (2, 1, 3, 0)}
    for d, slot in slots.items():
        links.send(slot, contrib.at[1 - c, ry.at(d)], mine_in.at[ry.at(d)], partner)

    def summed(d):
        o = ry.at(d)
        links.arrived(slots[d], 128)
        mine_sum[o] = contrib[c, o] + mine_in[o]

    ms = ReduceScatter(ry, lambda o, h: mine_sum.at[o, pl.ds(64 * h, 64)], land_m)
    summed(2)
    ms.step(1, 0)
    summed(1)
    summed(3)
    ms.step(1, 1)
    summed(0)
    ms.step(2, 0)
    halves = ms.final()
    for h in (0, 1):
        merged[c, y, pl.ds(64 * h, 64)] = halves[h]
    rows = merged[c, y]

    outer[...] = tn(rows, rows).reshape(2, NY, 32, 256)
    slot = links.slot()
    links.send(slot, outer.at[1 - c], outer_in, partner)
    links.arrived(slot, 128)
    outer_sum[...] = outer[c] + outer_in[...]
    gs = Direct(ry, lambda o: outer_sum.at[o], lambda o, d: from_y.at[o])
    mg = AllGather(ry, lambda o: merged.at[c, o], lambda o, h: merged.at[c, o, pl.ds(64 * h, 64)])
    from_y[y] = outer_sum[y]
    gs.final()
    mg.step(1)
    over_x[x] = (from_y[0] + from_y[1]) + (from_y[2] + from_y[3])
    Direct(rx, lambda o: over_x.at[x], lambda o, d: over_x.at[o]).final()
    over_z[z] = (over_x[0] + over_x[1]) + (over_x[2] + over_x[3])
    gz = Direct(rz, lambda o: over_z.at[z], lambda o, d: over_z.at[o])
    mg.step(2)
    mg.final()
    slot = links.slot()
    links.send(slot, merged.at[c], merged.at[c], partner)
    gz.final()
    acc = over_z[0]
    for i in range(1, NZ):
        acc = acc + over_z[i]
    gram[c, y] = acc
    gy = Direct(ry, lambda o: gram.at[c, y], lambda o, d: gram.at[c, o])
    links.arrived(slot, 512)
    put_merged = pltpu.make_async_copy(merged, merged_out, out_sems.at[1])
    put_merged.start()
    gy.final()
    last = links.slot()
    links.send(last, gram.at[c], gram.at[c], partner)
    links.arrived(last, 128)
    put_gram = pltpu.make_async_copy(gram, gram_out, out_sems.at[2])
    put_gram.start()
    put_loadings.wait()
    put_merged.wait()
    links.drain()
    put_gram.wait()


PANEL = 32


def panel_inverse(tiles, lane0):
    groups = PANEL // 8
    sub = lax.broadcasted_iota(jnp.int32, (8, 128), 0)
    lane = lax.broadcasted_iota(jnp.int32, (8, 128), 1)

    def spread(tile, s):
        return jnp.broadcast_to(tile[s:s + 1, :], (8, 128))

    cols = [{g: jnp.broadcast_to(tiles[g][:, lane0 + j:lane0 + j + 1], (8, 128)) for g in range(j // 8, groups)}
            for j in range(PANEL)]
    unit = [jnp.where(lane == sub + 8 * g, 1.0, 0.0).astype(F32) for g in range(groups)]
    pivots = [jnp.ones((8, 128), F32) for g in range(groups)]
    for k in range(PANEL):
        gk, sk = divmod(k, 8)
        pivot = spread(cols[k][gk], sk)
        inverse = 1.0 / pivot
        pivots[gk] = jnp.where(sub == sk, pivot, pivots[gk])
        mult = {g: cols[k][g] * inverse for g in range(gk, groups)}
        for j in range(k + 1, PANEL):
            gj, sj = divmod(j, 8)
            entry = spread(cols[k][gj], sj)
            for g in range(gj, groups):
                cols[j][g] = cols[j][g] - mult[g] * entry
        row = spread(unit[gk], sk)
        for g in range(gk, groups):
            m = jnp.where(sub > sk, mult[g], 0.0) if g == gk else mult[g]
            unit[g] = unit[g] - m * row
    return jnp.concatenate([unit[g] * lax.rsqrt(pivots[g]) for g in range(groups)], axis=0)[:, :PANEL]


def tn(a, b):
    return lax.dot_general(a, b, (((0,), (0,)), ((), ())), precision=HIGH, preferred_element_type=F32)


def factor_inverse(work, inverse, between):
    n = work.shape[0]
    for p in range(n // PANEL):
        r0 = p * PANEL
        lt = r0 // 128 * 128
        tiles = [work[r0 + 8 * g:r0 + 8 * g + 8, lt:lt + 128] for g in range(PANEL // 8)]
        block = panel_inverse(tiles, r0 - lt)
        col = lax.broadcasted_iota(jnp.int32, (PANEL, n), 1)
        row = lax.broadcasted_iota(jnp.int32, (PANEL, n), 0)
        here = (col >= r0) & (col < r0 + PANEL)
        wide = jnp.where(here, jnp.where(col == row + r0, 1.0, 0.0), work[r0:r0 + PANEL, :])
        u = nn(block, wide)
        inverse[r0:r0 + PANEL, :] = jnp.where(col < r0 + PANEL, u, 0.0)
        between(p)
        r1 = r0 + PANEL
        if r1 < n:
            base = r1 // 128 * 128
            upd = tn(u[:, base:], u)[r1 - base:]
            col = lax.broadcasted_iota(jnp.int32, (n - r1, n), 1)
            here = (col >= r0) & (col < r1)
            work[r1:, :] = jnp.where(here, 0.0, work[r1:, :]) - upd


def solve(root, gram, merged, loaded, updated, loadings, work, inverse, rows, passing, solved, sems):
    bring_gram = pltpu.make_async_copy(gram, work, sems.at[0])
    bring_rows = pltpu.make_async_copy(merged, rows, sems.at[1])
    bring = pltpu.make_async_copy(loaded, passing, sems.at[2])
    put = pltpu.make_async_copy(passing, loadings, sems.at[3])
    bring_gram.start()
    bring_rows.start()
    bring.start()
    bring_gram.wait()

    def between(panel):
        if panel == 2:
            bring.wait()
            put.start()

    factor_inverse(work, inverse, between)
    bring_rows.wait()
    puts = []
    for i in range(4):
        here = slice(256 * i, 256 * i + 256)
        solved[here, :] = nt(rows[here, :], inverse[...]) * root
        puts.append(pltpu.make_async_copy(solved.at[here], updated.at[here], sems.at[4 + i]))
        puts[-1].start()
    put.wait()
    for copy in puts:
        copy.wait()


def shards(sketched, widths, inv_factor, shared):
    total_rows = shared.shape[0] * lax.axis_size("sent")
    smem, hbm = (pl.BlockSpec(memory_space=m) for m in (pltpu.SMEM, pltpu.HBM))

    def buf(*shape):
        return pltpu.VMEM(shape, F32)

    sems = [pltpu.SemaphoreType.DMA((SEND_SEMS,)), pltpu.SemaphoreType.DMA((RECV_SEMS,))]

    def kernel_a(*refs):
        project(1.0 / math.sqrt(total_rows), *refs)

    loadings, merged, gram = pl.pallas_call(
        kernel_a,
        name="project",
        out_shape=(jax.ShapeDtypeStruct((3, 1024, 256), F32), jax.ShapeDtypeStruct((2, NY, 128, 256), F32),
                   jax.ShapeDtypeStruct((2, NY, 32, 256), F32)),
        in_specs=[smem, hbm, hbm, hbm],
        out_specs=(hbm, hbm, hbm),
        scratch_shapes=[
            pltpu.VMEM((3, 4, 1024, 256), BF16), pltpu.VMEM((1024, 256), BF16), pltpu.VMEM((256, 1024), BF16),
            buf(3, 2, 4, 8, 16, 256), buf(3, 2, 2, 2, 2, 4, 16, 256), buf(3, 2, 2, 2, 4, 8, 256),
            buf(3, 2, 2, 2, 4, 4, 8, 256), buf(3, 2, 2, 2, 2, 8, 256), buf(3, 2, 8, 16, 256), buf(3, 2, 4, 16, 256),
            buf(3, 2, 8, 16, 256), buf(3, 4, 64, 256), buf(3, 2, 32, 256),
            buf(3, 2, 2, 4, 16, 256), buf(3, 2, 4, 16, 256), buf(3, 2, 4, 16, 256), buf(3, 2, 2, 2, 2, 8, 256),
            buf(3, 2, 2, 4, 16, 256), buf(3, 2, 8, 16, 256), buf(3, 2, 2, 2, 4, 8, 256), buf(3, 2, 4, 8, 16, 256),
            buf(3, 1024, 256), buf(2, NY, 128, 256), buf(2, NY, 32, 256), buf(3, 2, 2, 8, 16, 256), buf(3, 2, 2, 4, 16, 256),
            buf(2, 4, 128, 256), buf(4, 128, 256), buf(4, 128, 256), buf(2, 2, 2, 64, 256), buf(2, 4, 32, 256),
            buf(4, 32, 256), buf(4, 32, 256), buf(4, 32, 256), buf(4, 32, 256), buf(8, 32, 256), *sems,
            pltpu.SemaphoreType.DMA((12,)), pltpu.SemaphoreType.DMA((2,)), pltpu.SemaphoreType.DMA((3,))],
        compiler_params=pltpu.CompilerParams(collective_id=0, has_side_effects=True, vmem_limit_bytes=58 * 2**20),
    )(widths, shared, inv_factor, sketched)
    merged, gram = merged.reshape(1024, 256), gram.reshape(256, 256)

    def kernel_c(*refs):
        solve(math.sqrt(total_rows), *refs)

    updated, loadings = pl.pallas_call(
        kernel_c,
        name="solve",
        out_shape=(jax.ShapeDtypeStruct((1024, 256), F32), jax.ShapeDtypeStruct((3, 1024, 256), F32)),
        in_specs=[hbm, hbm, hbm],
        out_specs=(hbm, hbm),
        scratch_shapes=[buf(256, 256), buf(256, 256), buf(1024, 256), buf(3, 1024, 256), buf(1024, 256),
                        pltpu.SemaphoreType.DMA((8,))],
        compiler_params=pltpu.CompilerParams(vmem_limit_bytes=58 * 2**20),
    )(gram, merged, loadings)
    return (loadings, updated)


def solution(mesh):
    return jax.shard_map(
        shards,
        mesh=mesh,
        in_specs=(P("view", "sent", "col"), P("view"), P("view", "sent", "col"), P("sent", None)),
        out_specs=(P("view", "col", None), P("sent", None)),
        check_vma=False,
    )
```

time: 164 us -> 148 us (0.902)
  Pallas kernels: 160 us -> 147 us
  local copies, waits for them, and re-layouts: 2.82 us -> 0 us
    pallas_call x1, Pallas kernels: 149 us -> 135 us  [shards(): pl.pallas_call(kernel_a, name='project', out_shape=(jax.ShapeDtypeStruct(...]
    unnamed x6 -> x0, local copies, waits for them, and re-layouts: 2.82 us -> none
where the time goes in v5:
time: 148 us; the launch traced here: 147 us
  Pallas kernels  147 us (99%)
    pallas_call x1, Pallas kernels, shards(): pl.pallas_call(kernel_a, name='project', out_shape=(jax.ShapeDtypeStruct(...  135 us
    pallas_call x1, Pallas kernels, shards(): pl.pallas_call(kernel_c, name='solve', out_shape=(jax.ShapeDtypeStruct((1...  12 us

profile of v5, /device:TPU:1, one launch (start us, length us, event | category | flops | bytes accessed | tf_op | source)
XLA Modules:
  0.0 147.4 jit_solution(12840361757898759999)
XLA Ops:
  0.6 134.6 %project.1 = (f32[3,1024,256]{2,1,0:T(8,128)}, f32[2,4,128,256]{3,2,1,0:T(8,128)}, f32[2,4,32,256]{3,2,1,0:T(8,128)}) custom-call(s32[3]{0:T(128)} %refs_0_.1, bf16[1024,256]{1,0:T(8,128)(2,1)} %refs_1_.1, f32[3,64,1024]{2,1,0:T(8,128)} %refs_2_.1, bf16[3,1024,1024]{2,1,0:T(8,128)(2,1)} %refs_3_.1), custom_call_target="tpu_custom_call" | custom-call | tf_op jit(solution)/shard_map/project/pallas_call | solution.py:561
  135.2 12.0 %solve.1 = (f32[1024,256]{1,0:T(8,128)}, f32[3,1024,256]{2,1,0:T(8,128)}) custom-call(f32[256,256]{1,0:T(8,128)} %bitcast.3, f32[1024,256]{1,0:T(8,128)} %bitcast.2, f32[3,1024,256]{2,1,0:T(8,128)} %get-tuple-element.9.refs_2_), custom_call_target="tpu_custom_call" | custom-call | tf_op jit(solution)/shard_map/solve/pallas_call | solution.py:586

commit v6 on v5

--- a/solution.py
+++ b/solution.py
@@ -227,20 +227,20 @@
 
 
 CHAINS = (
-    (0, 0, 0.02, "z", "z", (True, False, True, True, True, False)),
-    (0, 1, 1.01, "x", "z", (True, False, False, False, True, False)),
-    (1, 0, 2.03, "x", "x", (False, True, True, True, False, True)),
-    (1, 1, 2.05, "z", "z", (False, True, False, True, True, False)),
-    (2, 0, 10.04, "z", "x", (True, True, True, True, True, True)),
-    (2, 1, 11.0, "x", "x", (False, True, True, False, True, True)),
+    (0, 0, 0.0, "z", "z", (True, True, True, True, True, False)),
+    (0, 1, 0.03, "x", "z", (False, True, True, True, True, False)),
+    (1, 0, 1.02, "x", "x", (False, True, True, True, True, True)),
+    (1, 1, 1.05, "z", "x", (True, False, True, True, True, True)),
+    (2, 0, 2.04, "z", "z", (True, True, True, True, True, False)),
+    (2, 1, 10.01, "z", "x", (True, True, True, True, True, True)),
 )
-INV_START = 15.0
+INV_START = 12.0
 
 
 def project(scale, widths, shared, inv, sketched, loadings, merged_out, gram_out,
             feats, sharedH, sharedT, terms, land_x, land_xz, land_z, land_zx, quarter, slab, proj, invx, hop,
             part, part_in, part_sum, land_h, half, back, land_b, loadT, stage, merged, gram, land_8, land_4,
-            contrib, mine_in, mine_sum, land_m, outer, outer_in, outer_sum, from_y, over_x, over_z,
+            contrib, mine_in, mine_sum, land_m, outer, outer_in, outer_sum, from_y, sum_y, over_x, over_z,
             send_sems, recv_sems, feat_sems, own_sems, out_sems):
     y, x, z, c = place()
     links = Links(send_sems, recv_sems, stage)
@@ -429,19 +429,22 @@
     from_y[y] = outer_sum[y]
     gs.final()
     mg.step(1)
-    over_x[x] = (from_y[0] + from_y[1]) + (from_y[2] + from_y[3])
-    Direct(rx, lambda o: over_x.at[x], lambda o, d: over_x.at[o]).final()
+    sum_y[...] = ((from_y[0] + from_y[1]) + (from_y[2] + from_y[3])).reshape(NX, 8, 256)
+    over_x[x] = sum_y[x]
+    Direct(rx, lambda o: sum_y.at[o], lambda o, d: over_x.at[o]).final()
     over_z[z] = (over_x[0] + over_x[1]) + (over_x[2] + over_x[3])
     gz = Direct(rz, lambda o: over_z.at[z], lambda o, d: over_z.at[o])
     mg.step(2)
-    mg.final()
-    slot = links.slot()
-    links.send(slot, merged.at[c], merged.at[c], partner)
     gz.final()
     acc = over_z[0]
     for i in range(1, NZ):
         acc = acc + over_z[i]
-    gram[c, y] = acc
+    gram[c, y, x] = acc
+    gx = Direct(rx, lambda o: gram.at[c, y, x], lambda o, d: gram.at[c, y, o])
+    mg.final()
+    slot = links.slot()
+    links.send(slot, merged.at[c], merged.at[c], partner)
+    gx.final()
     gy = Direct(ry, lambda o: gram.at[c, y], lambda o, d: gram.at[c, o])
     links.arrived(slot, 512)
     put_merged = pltpu.make_async_copy(merged, merged_out, out_sems.at[1])
@@ -562,7 +565,7 @@
         kernel_a,
         name="project",
         out_shape=(jax.ShapeDtypeStruct((3, 1024, 256), F32), jax.ShapeDtypeStruct((2, NY, 128, 256), F32),
-                   jax.ShapeDtypeStruct((2, NY, 32, 256), F32)),
+                   jax.ShapeDtypeStruct((2, NY, NX, 8, 256), F32)),
         in_specs=[smem, hbm, hbm, hbm],
         out_specs=(hbm, hbm, hbm),
         scratch_shapes=[
@@ -572,9 +575,9 @@
             buf(3, 2, 8, 16, 256), buf(3, 4, 64, 256), buf(3, 2, 32, 256),
             buf(3, 2, 2, 4, 16, 256), buf(3, 2, 4, 16, 256), buf(3, 2, 4, 16, 256), buf(3, 2, 2, 2, 2, 8, 256),
             buf(3, 2, 2, 4, 16, 256), buf(3, 2, 8, 16, 256), buf(3, 2, 2, 2, 4, 8, 256), buf(3, 2, 4, 8, 16, 256),
-            buf(3, 1024, 256), buf(2, NY, 128, 256), buf(2, NY, 32, 256), buf(3, 2, 2, 8, 16, 256), buf(3, 2, 2, 4, 16, 256),
+            buf(3, 1024, 256), buf(2, NY, 128, 256), buf(2, NY, NX, 8, 256), buf(3, 2, 2, 8, 16, 256), buf(3, 2, 2, 4, 16, 256),
             buf(2, 4, 128, 256), buf(4, 128, 256), buf(4, 128, 256), buf(2, 2, 2, 64, 256), buf(2, 4, 32, 256),
-            buf(4, 32, 256), buf(4, 32, 256), buf(4, 32, 256), buf(4, 32, 256), buf(8, 32, 256), *sems,
+            buf(4, 32, 256), buf(4, 32, 256), buf(4, 32, 256), buf(4, 8, 256), buf(4, 8, 256), buf(8, 8, 256), *sems,
             pltpu.SemaphoreType.DMA((12,)), pltpu.SemaphoreType.DMA((2,)), pltpu.SemaphoreType.DMA((3,))],
         compiler_params=pltpu.CompilerParams(collective_id=0, has_side_effects=True, vmem_limit_bytes=58 * 2**20),
     )(widths, shared, inv_factor, sketched)

time: 148 us -> 143 us (0.966)
  Pallas kernels: 147 us -> 142 us
    pallas_call x1, Pallas kernels: 135 us -> 130 us  [shards(): pl.pallas_call(kernel_a, name='project', out_shape=(jax.ShapeDtypeStruct(...]
where the time goes in v6:
time: 143 us
  Pallas kernels  142 us (99%)
    pallas_call x1, Pallas kernels, shards(): pl.pallas_call(kernel_a, name='project', out_shape=(jax.ShapeDtypeStruct(...  130 us
    pallas_call x1, Pallas kernels, shards(): pl.pallas_call(kernel_c, name='solve', out_shape=(jax.ShapeDtypeStruct((1...  12 us

profile of v6, /device:TPU:1, one launch (start us, length us, event | category | flops | bytes accessed | tf_op | source)
XLA Modules:
  0.0 142.8 jit_solution(5988064982515438446)
XLA Ops:
  0.6 130.0 %project.1 = (f32[3,1024,256]{2,1,0:T(8,128)}, f32[2,4,128,256]{3,2,1,0:T(8,128)}, f32[2,4,4,8,256]{4,3,2,1,0:T(8,128)}) custom-call(s32[3]{0:T(128)} %refs_0_.1, bf16[1024,256]{1,0:T(8,128)(2,1)} %refs_1_.1, f32[3,64,1024]{2,1,0:T(8,128)} %refs_2_.1, bf16[3,1024,1024]{2,1,0:T(8,128)(2,1)} %refs_3_.1), custom_call_target="tpu_custom_call" | custom-call | tf_op jit(solution)/shard_map/project/pallas_call | solution.py:564
  130.6 12.0 %solve.1 = (f32[1024,256]{1,0:T(8,128)}, f32[3,1024,256]{2,1,0:T(8,128)}) custom-call(f32[256,256]{1,0:T(8,128)} %bitcast.3, f32[1024,256]{1,0:T(8,128)} %bitcast.2, f32[3,1024,256]{2,1,0:T(8,128)} %get-tuple-element.9.refs_2_), custom_call_target="tpu_custom_call" | custom-call | tf_op jit(solution)/shard_map/solve/pallas_call | solution.py:589

commit v7 on v6

--- a/solution.py
+++ b/solution.py
@@ -12,14 +12,14 @@
 F32 = jnp.float32
 BF16 = jnp.bfloat16
 NX, NZ, NY = 4, 8, 4
-SEND_SEMS, RECV_SEMS = 40, 224
+SEND_SEMS, RECV_SEMS = 12, 157
 
 
 class Clock:
     def __init__(self):
         self.now, self.busy, self.flows = 0.0, {}, []
 
-    def sent(self, axis, kib, latency=2.4):
+    def sent(self, axis, kib, latency=3.0):
         self.busy[axis] = max(self.now, self.busy.get(axis, 0.0)) + kib * 0.0225
         return self.busy[axis] + latency
 
@@ -320,8 +320,7 @@
         block = loadT[v, k, q].reshape(128, 256).T
         stage[v, columns(q), 128 * k:128 * k + 128] = block
         product = jnp.dot(feats[v, q], block.astype(BF16), preferred_element_type=F32).reshape(2, NY, 128, 128)
-        here = slice(128 * k, 128 * k + 128)
-        contrib[:, :, :, here] = contrib[:, :, :, here] + product if k in used else product
+        contrib[k] = contrib[k] + product if k in used else product
         used.append(k)
 
     made = set()
@@ -335,6 +334,32 @@
             terms[v, :, q] = jnp.dot(sharedT[...], feats[v, q], preferred_element_type=F32).reshape(2, NZ, 16, 256)
         if len(made) == 1:
             pl.semaphore_wait(barrier, len(peers))
+
+    def merge_flow(k):
+        slots = {d: links.slot() for d in (2, 1, 3, 0)}
+        for d, slot in slots.items():
+            links.send(slot, contrib.at[k, 1 - c, ry.at(d)], mine_in.at[k, ry.at(d)], partner)
+        yield clock.now + 1.55
+
+        def summed(d):
+            o = ry.at(d)
+            links.arrived(slots[d], 64)
+            mine_sum[k, o] = contrib[k, c, o] + mine_in[k, o]
+
+        ms = ReduceScatter(ry, lambda o, h: mine_sum.at[k, o, pl.ds(64 * h, 64)], land_m.at[k])
+        summed(2)
+        due = ms.step(1, 0)
+        summed(1)
+        summed(3)
+        ms.step(1, 1)
+        summed(0)
+        yield due
+        yield ms.step(2, 0)
+        halves = ms.final()
+        for h in (0, 1):
+            merged[c, y, pl.ds(64 * h, 64), 128 * k:128 * k + 128] = halves[h]
+
+    finished = []
 
     def chain(v, k, first, last, direct):
         make_terms(v)
@@ -389,6 +414,9 @@
 
             yield from AllGather(
                 rx, lambda o: loadT.at[v, k, o], lambda o, h: loadT.at[v, k, o, pl.ds(4 * h, 4)]).flow(reached)
+        finished.append(k)
+        if finished.count(k) == 3:
+            yield from merge_flow(k)
 
     for v, k, start, first, last, direct in CHAINS:
         clock.add(start, chain(v, k, first, last, direct))
@@ -397,26 +425,6 @@
     put_loadings = pltpu.make_async_copy(stage, loadings, out_sems.at[0])
     put_loadings.start()
 
-    slots = {d: links.slot() for d in (2, 1, 3, 0)}
-    for d, slot in slots.items():
-        links.send(slot, contrib.at[1 - c, ry.at(d)], mine_in.at[ry.at(d)], partner)
-
-    def summed(d):
-        o = ry.at(d)
-        links.arrived(slots[d], 128)
-        mine_sum[o] = contrib[c, o] + mine_in[o]
-
-    ms = ReduceScatter(ry, lambda o, h: mine_sum.at[o, pl.ds(64 * h, 64)], land_m)
-    summed(2)
-    ms.step(1, 0)
-    summed(1)
-    summed(3)
-    ms.step(1, 1)
-    summed(0)
-    ms.step(2, 0)
-    halves = ms.final()
-    for h in (0, 1):
-        merged[c, y, pl.ds(64 * h, 64)] = halves[h]
     rows = merged[c, y]
 
     outer[...] = tn(rows, rows).reshape(2, NY, 32, 256)
@@ -576,7 +584,7 @@
             buf(3, 2, 2, 4, 16, 256), buf(3, 2, 4, 16, 256), buf(3, 2, 4, 16, 256), buf(3, 2, 2, 2, 2, 8, 256),
             buf(3, 2, 2, 4, 16, 256), buf(3, 2, 8, 16, 256), buf(3, 2, 2, 2, 4, 8, 256), buf(3, 2, 4, 8, 16, 256),
             buf(3, 1024, 256), buf(2, NY, 128, 256), buf(2, NY, NX, 8, 256), buf(3, 2, 2, 8, 16, 256), buf(3, 2, 2, 4, 16, 256),
-            buf(2, 4, 128, 256), buf(4, 128, 256), buf(4, 128, 256), buf(2, 2, 2, 64, 256), buf(2, 4, 32, 256),
+            buf(2, 2, 4, 128, 128), buf(2, 4, 128, 128), buf(2, 4, 128, 128), buf(2, 2, 2, 2, 64, 128), buf(2, 4, 32, 256),
             buf(4, 32, 256), buf(4, 32, 256), buf(4, 32, 256), buf(4, 8, 256), buf(4, 8, 256), buf(8, 8, 256), *sems,
             pltpu.SemaphoreType.DMA((12,)), pltpu.SemaphoreType.DMA((2,)), pltpu.SemaphoreType.DMA((3,))],
         compiler_params=pltpu.CompilerParams(collective_id=0, has_side_effects=True, vmem_limit_bytes=58 * 2**20),

time: 143 us -> 141 us (0.986)
  Pallas kernels: 142 us -> 140 us
    pallas_call x1, Pallas kernels: 130 us -> 128 us  [shards(): pl.pallas_call(kernel_a, name='project', out_shape=(jax.ShapeDtypeStruct(...]
where the time goes in v7:
time: 141 us
  Pallas kernels  140 us (99%)
    pallas_call x1, Pallas kernels, shards(): pl.pallas_call(kernel_a, name='project', out_shape=(jax.ShapeDtypeStruct(...  128 us
    pallas_call x1, Pallas kernels, shards(): pl.pallas_call(kernel_c, name='solve', out_shape=(jax.ShapeDtypeStruct((1...  12 us

profile of v7, /device:TPU:1, one launch (start us, length us, event | category | flops | bytes accessed | tf_op | source)
XLA Modules:
  0.0 140.8 jit_solution(15130067522080390349)
XLA Ops:
  0.6 128.0 %project.1 = (f32[3,1024,256]{2,1,0:T(8,128)}, f32[2,4,128,256]{3,2,1,0:T(8,128)}, f32[2,4,4,8,256]{4,3,2,1,0:T(8,128)}) custom-call(s32[3]{0:T(128)} %refs_0_.1, bf16[1024,256]{1,0:T(8,128)(2,1)} %refs_1_.1, f32[3,64,1024]{2,1,0:T(8,128)} %refs_2_.1, bf16[3,1024,1024]{2,1,0:T(8,128)(2,1)} %refs_3_.1), custom_call_target="tpu_custom_call" | custom-call | tf_op jit(solution)/shard_map/project/pallas_call | solution.py:572
  128.6 12.0 %solve.1 = (f32[1024,256]{1,0:T(8,128)}, f32[3,1024,256]{2,1,0:T(8,128)}) custom-call(f32[256,256]{1,0:T(8,128)} %bitcast.3, f32[1024,256]{1,0:T(8,128)} %bitcast.2, f32[3,1024,256]{2,1,0:T(8,128)} %get-tuple-element.9.refs_2_), custom_call_target="tpu_custom_call" | custom-call | tf_op jit(solution)/shard_map/solve/pallas_call | solution.py:597

commit v8 on v7

--- a/solution.py
+++ b/solution.py
@@ -19,7 +19,7 @@
     def __init__(self):
         self.now, self.busy, self.flows = 0.0, {}, []
 
-    def sent(self, axis, kib, latency=3.0):
+    def sent(self, axis, kib, latency=3.5):
         self.busy[axis] = max(self.now, self.busy.get(axis, 0.0)) + kib * 0.0225
         return self.busy[axis] + latency
 

time: 141 us -> 144 us (1.021)
  Pallas kernels: 140 us -> 143 us
    pallas_call x1, Pallas kernels: 128 us -> 131 us  [shards(): pl.pallas_call(kernel_a, name='project', out_shape=(jax.ShapeDtypeStruct(...]
where the time goes in v8:
time: 144 us
  Pallas kernels  143 us (99%)
    pallas_call x1, Pallas kernels, shards(): pl.pallas_call(kernel_a, name='project', out_shape=(jax.ShapeDtypeStruct(...  131 us
    pallas_call x1, Pallas kernels, shards(): pl.pallas_call(kernel_c, name='solve', out_shape=(jax.ShapeDtypeStruct((1...  12 us

profile of v8, /device:TPU:1, one launch (start us, length us, event | category | flops | bytes accessed | tf_op | source)
XLA Modules:
  0.0 143.9 jit_solution(7859823082524577319)
XLA Ops:
  0.6 131.1 %project.1 = (f32[3,1024,256]{2,1,0:T(8,128)}, f32[2,4,128,256]{3,2,1,0:T(8,128)}, f32[2,4,4,8,256]{4,3,2,1,0:T(8,128)}) custom-call(s32[3]{0:T(128)} %refs_0_.1, bf16[1024,256]{1,0:T(8,128)(2,1)} %refs_1_.1, f32[3,64,1024]{2,1,0:T(8,128)} %refs_2_.1, bf16[3,1024,1024]{2,1,0:T(8,128)(2,1)} %refs_3_.1), custom_call_target="tpu_custom_call" | custom-call | tf_op jit(solution)/shard_map/project/pallas_call | solution.py:572
  131.7 12.0 %solve.1 = (f32[1024,256]{1,0:T(8,128)}, f32[3,1024,256]{2,1,0:T(8,128)}) custom-call(f32[256,256]{1,0:T(8,128)} %bitcast.3, f32[1024,256]{1,0:T(8,128)} %bitcast.2, f32[3,1024,256]{2,1,0:T(8,128)} %get-tuple-element.9.refs_2_), custom_call_target="tpu_custom_call" | custom-call | tf_op jit(solution)/shard_map/solve/pallas_call | solution.py:597
